TPU v7x, 512 devices: a whole 4x8x8 slice. The times are simulated.
512 devices in a mesh: layer: 16 (over x_hi, z), row: 8 (over y), col: 4 (over x_lo, core).
Axes of the slice: x: 4 (x_hi: 2, x_lo: 2; x = x_hi * 2 + x_lo), y: 8, z: 8, core: 2. Of those that a mesh axis runs over, the one named last changes fastest.
Arguments:
- sources: bfloat16 [16, 64, 16, 16, 128], P('layer', None, 'row', 'col'), may hold values from -3 to 3
- adjoint_sources: bfloat16 [16, 64, 16, 16, 128], P('layer', None, 'row', 'col'), may hold values from -3 to 3
- blocks: bfloat16 [16, 16, 16, 9, 128, 128], P('layer', 'row', 'col'), may hold values from -0.2 to 1.4
- pattern: int32 [16, 16, 16, 9], P('layer', 'row', 'col'), may hold values 0 or 1
- coupling: float32 [4], replicated, may hold values from 0.7 to 0.9
- layer_group: int32 [16], replicated, may hold values from 0 to 3
- port_cells: int32 [64], replicated, may hold values from 0 to 32767
Outputs:
- forward_field: bfloat16 [16, 64, 16, 16, 128], P('layer', None, 'row', 'col')
- adjoint_field: bfloat16 [16, 64, 16, 16, 128], P('layer', None, 'row', 'col')
- gradient: float32 [4, 16, 16, 128], P(None, 'row', 'col')
All inputs are finite; a program needn't handle non-finite values. No bound on the sum of `pattern` on one device may be relied on, other than what follows from the above.
Results may differ from a plain program's by a relative error of at most 0.01.
Values may be sent and summed in bfloat16 or wider, within the bound.
A program may use at most 64 MiB of HBM per device.

v0:
```python
import jax
import jax.numpy as jnp
from jax import lax
from jax.sharding import PartitionSpec as P

port_strength = 4.0
intersection_scale = 0.125


def extended(array, sides, width):
    for axis, dim in sides:
        peers, length = (lax.axis_size(axis), array.shape[dim])
        up = [(i, (i + 1) % peers) for i in range(peers - 1)]
        down = [(j, i) for i, j in up]
        last = lax.slice_in_dim(array, length - width, length, axis=dim)
        initial = lax.slice_in_dim(array, 0, width, axis=dim)
        before = lax.ppermute(last, axis, up)
        after = lax.ppermute(initial, axis, down)
        array = jnp.concatenate([before, array, after], axis=dim)
    return array


def shifted(block, axis, distance):
    devices = range(lax.axis_size(axis))
    route = [(i - distance, i) for i in devices if i - distance in devices]
    return lax.ppermute(block, axis, route)


def local(sources, adjoint_sources, blocks, pattern, coupling, layer_group, port_cells):
    port_count = sources.shape[1]
    tiles_x = sources.shape[2]
    tiles_y = sources.shape[3]
    tile_cells = sources.shape[4]
    groups = coupling.shape[0]
    layer_count = lax.axis_size("layer")
    layer_pos = lax.axis_index("layer")
    row_pos = lax.axis_index("row")
    col_pos = lax.axis_index("col")
    member = (layer_group[:, None] == jnp.arange(groups, dtype=jnp.int32)[None, :]).astype(
        jnp.float32
    )
    kappa = jnp.dot(member, coupling, precision=lax.Precision.HIGHEST)
    kappa_own = lax.dynamic_index_in_dim(kappa, layer_pos, 0, keepdims=False)
    kappa_next = lax.dynamic_index_in_dim(
        kappa, jnp.minimum(layer_pos + 1, layer_count - 1), 0, keepdims=False
    )
    tiles_y_total = tiles_y * lax.axis_size("col")
    tile_xpos = row_pos * tiles_x + jnp.arange(tiles_x, dtype=jnp.int32)
    tile_ypos = col_pos * tiles_y + jnp.arange(tiles_y, dtype=jnp.int32)
    tile_ids = tile_xpos[:, None] * tiles_y_total + tile_ypos[None, :]
    cell_ids = (
        tile_ids[:, :, None] * tile_cells + jnp.arange(tile_cells, dtype=jnp.int32)[None, None, :]
    )
    port_map = (cell_ids[None] == port_cells[:, None, None, None]).astype(
        jnp.float32
    ) * port_strength
    first_flag = jnp.where(layer_pos == 0, 1.0, 0.0).astype(jnp.float32)
    last_flag = jnp.where(layer_pos == layer_count - 1, 1.0, 0.0).astype(jnp.float32)
    forward_rhs = sources[0].astype(jnp.float32) + first_flag * port_map
    adjoint_rhs = adjoint_sources[0].astype(jnp.float32) + last_flag * port_map
    front_blocks = blocks[0]
    front_mask = pattern[0].astype(jnp.float32)

    def apply_front(stacked):
        padded = extended(stacked, (("row", 1), ("col", 2)), 1)
        summed = jnp.zeros(stacked.shape, jnp.float32)
        for offset in range(9):
            step_x = offset // 3 - 1
            step_y = offset % 3 - 1
            beside = padded[
                :, 1 + step_x : 1 + step_x + tiles_x, 1 + step_y : 1 + step_y + tiles_y, :
            ]
            product_term = jnp.einsum(
                "pijc,ijcd->pijd",
                beside,
                front_blocks[:, :, offset],
                preferred_element_type=jnp.float32,
            )
            summed = summed + front_mask[None, :, :, offset, None] * product_term
        return summed

    def advance(forward_prev, adjoint_prev, forward_part, adjoint_part):
        forward_in = shifted(forward_prev, "layer", 1)
        adjoint_in = shifted(adjoint_prev, "layer", -1)
        forward_wave = (forward_part + kappa_own * forward_in.astype(jnp.float32)).astype(
            jnp.bfloat16
        )
        adjoint_wave = (adjoint_part + kappa_next * adjoint_in.astype(jnp.float32)).astype(
            jnp.bfloat16
        )
        rows_forward = forward_wave.shape[0]
        result = apply_front(jnp.concatenate([forward_wave, adjoint_wave], 0)).astype(jnp.bfloat16)
        return (result[:rows_forward], result[rows_forward:])

    adjoint_layer = layer_count - 1 - layer_pos
    empty = jnp.zeros((port_count, tiles_x, tiles_y, tile_cells), jnp.bfloat16)

    def section_step(step_index, state_pair):
        forward_now, adjoint_now = state_pair
        forward_new, adjoint_new = advance(forward_now, adjoint_now, forward_rhs, adjoint_rhs)
        forward_now = jnp.where(step_index == layer_pos, forward_new, forward_now)
        adjoint_now = jnp.where(step_index == adjoint_layer, adjoint_new, adjoint_now)
        return (forward_now, adjoint_now)

    forward_field, adjoint_field = lax.fori_loop(0, layer_count, section_step, (empty, empty))
    intersection = (
        jnp.sum(forward_field.astype(jnp.float32) * adjoint_field.astype(jnp.float32), axis=0)
        * intersection_scale
    )
    own_group = lax.dynamic_index_in_dim(layer_group, layer_pos, 0, keepdims=False)
    selector = (jnp.arange(groups, dtype=jnp.int32) == own_group).astype(jnp.float32)
    contribution = selector[:, None, None, None] * intersection[None]
    gradient = lax.psum(contribution, "layer")
    return (forward_field[None], adjoint_field[None], gradient)


def solution(mesh):
    placed = (
        P("layer", None, "row", "col", None),
        P("layer", None, "row", "col", None),
        P("layer", "row", "col", None, None, None),
        P("layer", "row", "col", None),
        P(),
        P(),
        P(),
    )
    return jax.shard_map(
        local,
        mesh=mesh,
        in_specs=placed,
        out_specs=(
            P("layer", None, "row", "col", None),
            P("layer", None, "row", "col", None),
            P(None, "row", "col", None),
        ),
        check_vma=False,
    )
```

profile of v0, /device:TPU:38, one launch (start us, length us, event | category | flops | bytes accessed | tf_op | source)
XLA Modules:
  0.0 630.1 jit_solution(2605185568363795545)
XLA Ops:
  6.1 542.7 %while.16 = (s32[]{:T(128)}, bf16[64,2,4,128]{3,0,2,1:T(8,128)(2,1)S(1)}, bf16[64,2,4,128]{3,0,2,1:T(8,128)(2,1)S(1)}, s32[]{:T(128)}, f32[2,4,9]{1,0,2:T(2,128)...) while((s32[]{:T(128)}, ...), condition=%wide.region_1.2_spmd.clone, body=%wide.region_0.1_spmd.clone.sunk | while | flops 329383936 | bytes 22816724 | solution.py:105
  6.7 4.3 collective-permute-start
  11.0 9.4 %collective-permute-start.1 = (bf16[64,2,4,128]{3,0,2,1:T(8,128)(2,1)S(1)}, bf16[64,2,4,128]{3,0,2,1:T(8,128)(2,1)S(1)}, u32[]{:S(2)}, u32[]{:S(2)}) collective-permute-start(bf16[64,2,4,128]{3,0,2,1:T(8,128)(2,1)S(1)} %broadcast_select_fusion.5), channel_id=1, source_target_pairs={{32,0},{64,32},{96,64},{128,96},{160,128},{192,160},{224,192},{256... | collective-permute-start | bytes 393224 | tf_op jit(solution)/shard_map/while/body/eval_jaxpr/ppermute | solution.py:26
  26.3 3.5 collective-permute-start.3
  30.8 3.6 collective-permute-done.3
  39.2 3.4 collective-permute-done.5
  46.8 8.0 %collective-permute-start.1 = (bf16[64,2,4,128]{3,0,2,1:T(8,128)(2,1)S(1)}, bf16[64,2,4,128]{3,0,2,1:T(8,128)(2,1)S(1)}, u32[]{:S(2)}, u32[]{:S(2)}) collective-permute-start(bf16[64,2,4,128]{3,0,2,1:T(8,128)(2,1)S(1)} %broadcast_select_fusion.5), channel_id=1, source_target_pairs={{32,0},{64,32},{96,64},{128,96},{160,128},{192,160},{224,192},{256... | collective-permute-start | bytes 393224 | tf_op jit(solution)/shard_map/while/body/eval_jaxpr/ppermute | solution.py:26
  59.9 3.9 collective-permute-start.3
  64.9 3.1 collective-permute-done.3
  72.8 3.4 collective-permute-done.5
  80.5 8.0 %collective-permute-start.1 = (bf16[64,2,4,128]{3,0,2,1:T(8,128)(2,1)S(1)}, bf16[64,2,4,128]{3,0,2,1:T(8,128)(2,1)S(1)}, u32[]{:S(2)}, u32[]{:S(2)}) collective-permute-start(bf16[64,2,4,128]{3,0,2,1:T(8,128)(2,1)S(1)} %broadcast_select_fusion.5), channel_id=1, source_target_pairs={{32,0},{64,32},{96,64},{128,96},{160,128},{192,160},{224,192},{256... | collective-permute-start | bytes 393224 | tf_op jit(solution)/shard_map/while/body/eval_jaxpr/ppermute | solution.py:26
  93.6 3.9 collective-permute-start.3
  98.5 3.1 collective-permute-done.3
  106.5 3.4 collective-permute-done.5
  114.1 8.0 %collective-permute-start.1 = (bf16[64,2,4,128]{3,0,2,1:T(8,128)(2,1)S(1)}, bf16[64,2,4,128]{3,0,2,1:T(8,128)(2,1)S(1)}, u32[]{:S(2)}, u32[]{:S(2)}) collective-permute-start(bf16[64,2,4,128]{3,0,2,1:T(8,128)(2,1)S(1)} %broadcast_select_fusion.5), channel_id=1, source_target_pairs={{32,0},{64,32},{96,64},{128,96},{160,128},{192,160},{224,192},{256... | collective-permute-start | bytes 393224 | tf_op jit(solution)/shard_map/while/body/eval_jaxpr/ppermute | solution.py:26
  127.2 3.9 collective-permute-start.3
  132.1 3.1 collective-permute-done.3
  140.1 3.4 collective-permute-done.5
  147.7 8.0 %collective-permute-start.1 = (bf16[64,2,4,128]{3,0,2,1:T(8,128)(2,1)S(1)}, bf16[64,2,4,128]{3,0,2,1:T(8,128)(2,1)S(1)}, u32[]{:S(2)}, u32[]{:S(2)}) collective-permute-start(bf16[64,2,4,128]{3,0,2,1:T(8,128)(2,1)S(1)} %broadcast_select_fusion.5), channel_id=1, source_target_pairs={{32,0},{64,32},{96,64},{128,96},{160,128},{192,160},{224,192},{256... | collective-permute-start | bytes 393224 | tf_op jit(solution)/shard_map/while/body/eval_jaxpr/ppermute | solution.py:26
  160.8 3.9 collective-permute-start.3
  165.7 3.1 collective-permute-done.3
  173.7 3.4 collective-permute-done.5
  181.3 8.1 %collective-permute-start.1 = (bf16[64,2,4,128]{3,0,2,1:T(8,128)(2,1)S(1)}, bf16[64,2,4,128]{3,0,2,1:T(8,128)(2,1)S(1)}, u32[]{:S(2)}, u32[]{:S(2)}) collective-permute-start(bf16[64,2,4,128]{3,0,2,1:T(8,128)(2,1)S(1)} %broadcast_select_fusion.5), channel_id=1, source_target_pairs={{32,0},{64,32},{96,64},{128,96},{160,128},{192,160},{224,192},{256... | collective-permute-start | bytes 393224 | tf_op jit(solution)/shard_map/while/body/eval_jaxpr/ppermute | solution.py:26
  194.5 3.9 collective-permute-start.3
  199.5 3.1 collective-permute-done.3
  207.4 3.4 collective-permute-done.5
  215.1 8.0 %collective-permute-start.1 = (bf16[64,2,4,128]{3,0,2,1:T(8,128)(2,1)S(1)}, bf16[64,2,4,128]{3,0,2,1:T(8,128)(2,1)S(1)}, u32[]{:S(2)}, u32[]{:S(2)}) collective-permute-start(bf16[64,2,4,128]{3,0,2,1:T(8,128)(2,1)S(1)} %broadcast_select_fusion.5), channel_id=1, source_target_pairs={{32,0},{64,32},{96,64},{128,96},{160,128},{192,160},{224,192},{256... | collective-permute-start | bytes 393224 | tf_op jit(solution)/shard_map/while/body/eval_jaxpr/ppermute | solution.py:26
  228.2 3.9 collective-permute-start.3
  233.1 3.1 collective-permute-done.3
  241.1 3.4 collective-permute-done.5
  248.7 8.0 %collective-permute-start.1 = (bf16[64,2,4,128]{3,0,2,1:T(8,128)(2,1)S(1)}, bf16[64,2,4,128]{3,0,2,1:T(8,128)(2,1)S(1)}, u32[]{:S(2)}, u32[]{:S(2)}) collective-permute-start(bf16[64,2,4,128]{3,0,2,1:T(8,128)(2,1)S(1)} %broadcast_select_fusion.5), channel_id=1, source_target_pairs={{32,0},{64,32},{96,64},{128,96},{160,128},{192,160},{224,192},{256... | collective-permute-start | bytes 393224 | tf_op jit(solution)/shard_map/while/body/eval_jaxpr/ppermute | solution.py:26
  261.8 3.9 collective-permute-start.3
  266.7 3.1 collective-permute-done.3
  274.7 3.4 collective-permute-done.5
  282.3 8.0 %collective-permute-start.1 = (bf16[64,2,4,128]{3,0,2,1:T(8,128)(2,1)S(1)}, bf16[64,2,4,128]{3,0,2,1:T(8,128)(2,1)S(1)}, u32[]{:S(2)}, u32[]{:S(2)}) collective-permute-start(bf16[64,2,4,128]{3,0,2,1:T(8,128)(2,1)S(1)} %broadcast_select_fusion.5), channel_id=1, source_target_pairs={{32,0},{64,32},{96,64},{128,96},{160,128},{192,160},{224,192},{256... | collective-permute-start | bytes 393224 | tf_op jit(solution)/shard_map/while/body/eval_jaxpr/ppermute | solution.py:26
  295.4 3.9 collective-permute-start.3
  300.3 3.1 collective-permute-done.3
  308.3 3.4 collective-permute-done.5
  315.9 8.0 %collective-permute-start.1 = (bf16[64,2,4,128]{3,0,2,1:T(8,128)(2,1)S(1)}, bf16[64,2,4,128]{3,0,2,1:T(8,128)(2,1)S(1)}, u32[]{:S(2)}, u32[]{:S(2)}) collective-permute-start(bf16[64,2,4,128]{3,0,2,1:T(8,128)(2,1)S(1)} %broadcast_select_fusion.5), channel_id=1, source_target_pairs={{32,0},{64,32},{96,64},{128,96},{160,128},{192,160},{224,192},{256... | collective-permute-start | bytes 393224 | tf_op jit(solution)/shard_map/while/body/eval_jaxpr/ppermute | solution.py:26
  329.0 3.9 collective-permute-start.3
  334.0 3.1 collective-permute-done.3
  341.9 3.4 collective-permute-done.5
  349.6 8.0 %collective-permute-start.1 = (bf16[64,2,4,128]{3,0,2,1:T(8,128)(2,1)S(1)}, bf16[64,2,4,128]{3,0,2,1:T(8,128)(2,1)S(1)}, u32[]{:S(2)}, u32[]{:S(2)}) collective-permute-start(bf16[64,2,4,128]{3,0,2,1:T(8,128)(2,1)S(1)} %broadcast_select_fusion.5), channel_id=1, source_target_pairs={{32,0},{64,32},{96,64},{128,96},{160,128},{192,160},{224,192},{256... | collective-permute-start | bytes 393224 | tf_op jit(solution)/shard_map/while/body/eval_jaxpr/ppermute | solution.py:26
  362.7 3.9 collective-permute-start.3
  367.6 3.1 collective-permute-done.3
  375.6 3.4 collective-permute-done.5
  383.2 8.0 %collective-permute-start.1 = (bf16[64,2,4,128]{3,0,2,1:T(8,128)(2,1)S(1)}, bf16[64,2,4,128]{3,0,2,1:T(8,128)(2,1)S(1)}, u32[]{:S(2)}, u32[]{:S(2)}) collective-permute-start(bf16[64,2,4,128]{3,0,2,1:T(8,128)(2,1)S(1)} %broadcast_select_fusion.5), channel_id=1, source_target_pairs={{32,0},{64,32},{96,64},{128,96},{160,128},{192,160},{224,192},{256... | collective-permute-start | bytes 393224 | tf_op jit(solution)/shard_map/while/body/eval_jaxpr/ppermute | solution.py:26
  396.3 3.9 collective-permute-start.3
  401.2 3.1 collective-permute-done.3
  409.2 3.4 collective-permute-done.5
  416.8 8.0 %collective-permute-start.1 = (bf16[64,2,4,128]{3,0,2,1:T(8,128)(2,1)S(1)}, bf16[64,2,4,128]{3,0,2,1:T(8,128)(2,1)S(1)}, u32[]{:S(2)}, u32[]{:S(2)}) collective-permute-start(bf16[64,2,4,128]{3,0,2,1:T(8,128)(2,1)S(1)} %broadcast_select_fusion.5), channel_id=1, source_target_pairs={{32,0},{64,32},{96,64},{128,96},{160,128},{192,160},{224,192},{256... | collective-permute-start | bytes 393224 | tf_op jit(solution)/shard_map/while/body/eval_jaxpr/ppermute | solution.py:26
  429.9 3.9 collective-permute-start.3
  434.9 3.1 collective-permute-done.3
  442.8 3.4 collective-permute-done.5
  450.4 8.0 %collective-permute-start.1 = (bf16[64,2,4,128]{3,0,2,1:T(8,128)(2,1)S(1)}, bf16[64,2,4,128]{3,0,2,1:T(8,128)(2,1)S(1)}, u32[]{:S(2)}, u32[]{:S(2)}) collective-permute-start(bf16[64,2,4,128]{3,0,2,1:T(8,128)(2,1)S(1)} %broadcast_select_fusion.5), channel_id=1, source_target_pairs={{32,0},{64,32},{96,64},{128,96},{160,128},{192,160},{224,192},{256... | collective-permute-start | bytes 393224 | tf_op jit(solution)/shard_map/while/body/eval_jaxpr/ppermute | solution.py:26
  463.5 3.9 collective-permute-start.3
  476.4 3.4 collective-permute-done.5
  484.1 8.0 %collective-permute-start.1 = (bf16[64,2,4,128]{3,0,2,1:T(8,128)(2,1)S(1)}, bf16[64,2,4,128]{3,0,2,1:T(8,128)(2,1)S(1)}, u32[]{:S(2)}, u32[]{:S(2)}) collective-permute-start(bf16[64,2,4,128]{3,0,2,1:T(8,128)(2,1)S(1)} %broadcast_select_fusion.5), channel_id=1, source_target_pairs={{32,0},{64,32},{96,64},{128,96},{160,128},{192,160},{224,192},{256... | collective-permute-start | bytes 393224 | tf_op jit(solution)/shard_map/while/body/eval_jaxpr/ppermute | solution.py:26
  497.2 3.9 collective-permute-start.3
  510.1 3.4 collective-permute-done.5
  517.7 8.0 %collective-permute-start.1 = (bf16[64,2,4,128]{3,0,2,1:T(8,128)(2,1)S(1)}, bf16[64,2,4,128]{3,0,2,1:T(8,128)(2,1)S(1)}, u32[]{:S(2)}, u32[]{:S(2)}) collective-permute-start(bf16[64,2,4,128]{3,0,2,1:T(8,128)(2,1)S(1)} %broadcast_select_fusion.5), channel_id=1, source_target_pairs={{32,0},{64,32},{96,64},{128,96},{160,128},{192,160},{224,192},{256... | collective-permute-start | bytes 393224 | tf_op jit(solution)/shard_map/while/body/eval_jaxpr/ppermute | solution.py:26
  530.8 3.9 collective-permute-start.3
  543.7 3.5 collective-permute-done.5
  550.8 78.3 %psum.7 = f32[4,2,4,128]{3,2,1,0:T(4,128)} all-reduce(f32[4,2,4,128]{3,2,1,0:T(4,128)S(1)} %broadcast_multiply_fusion), channel_id=1, replica_groups=mesh['layer'=16,'row'=8,'col'=4] {'layer'}, use_global_device_ids=true, to_apply=%region_3.4 | all-reduce | flops 4096 | bytes 32768 | tf_op jit(solution)/shard_map/psum | solution.py:113
  (424 shorter events, 256.4 us)
Async XLA Ops:
  6.7 15.5 %collective-permute-start = (bf16[64,2,4,128]{3,0,2,1:T(8,128)(2,1)}, bf16[64,2,4,128]{3,0,2,1:T(8,128)(2,1)S(1)}, u32[]{:S(2)}, u32[]{:S(2)}) collective-permute-start(bf16[64,2,4,128]{3,0,2,1:T(8,128)(2,1)} %broadcast_select_fusion.4), channel_id=1, source_target_pairs={{0,32},{32,64},{64,96},{96,128},{128,160},{160,192},{192,224},{224... | collective-permute-start | bytes 393224 | tf_op jit(solution)/shard_map/while/body/eval_jaxpr/ppermute | solution.py:26
  11.0 12.2 %collective-permute-start.1 = (bf16[64,2,4,128]{3,0,2,1:T(8,128)(2,1)S(1)}, bf16[64,2,4,128]{3,0,2,1:T(8,128)(2,1)S(1)}, u32[]{:S(2)}, u32[]{:S(2)}) collective-permute-start(bf16[64,2,4,128]{3,0,2,1:T(8,128)(2,1)S(1)} %broadcast_select_fusion.5), channel_id=1, source_target_pairs={{32,0},{64,32},{96,64},{128,96},{160,128},{192,160},{224,192},{256... | collective-permute-start | bytes 393224 | tf_op jit(solution)/shard_map/while/body/eval_jaxpr/ppermute | solution.py:26
  26.3 8.1 %collective-permute-start.3 = (bf16[128,1,4,128]{3,0,2,1:T(8,128)(2,1)S(1)}, bf16[128,1,4,128]{3,0,2,1:T(8,128)(2,1)S(1)}, u32[]{:S(2)}, u32[]{:S(2)}) collective-permute-start(bf16[128,1,4,128]{3,0,2,1:T(8,128)(2,1)S(1)} %get-tuple-element.364), channel_id=1, source_target_pairs={{0,4},{4,8},{8,12},{12,16},{16,20},{20,24},{24,28},{1,5},{5,9},{9,... | collective-permute-start | bytes 393224 | tf_op jit(solution)/shard_map/while/body/eval_jaxpr/ppermute | solution.py:17
  34.4 8.7 %collective-permute-start.4 = (bf16[128,4,1,128]{3,0,2,1:T(8,128)(2,1)S(1)}, bf16[128,4,1,128]{3,0,2,1:T(8,128)(2,1)S(1)}, u32[]{:S(2)}, u32[]{:S(2)}) collective-permute-start(bf16[128,4,1,128]{3,0,2,1:T(8,128)(2,1)S(1)} %get-tuple-element.365), channel_id=1, source_target_pairs={{1,0},{2,1},{3,2},{5,4},{6,5},{7,6},{9,8},{10,9},{11,10},{13,12},{... | collective-permute-start | bytes 393224 | tf_op jit(solution)/shard_map/while/body/eval_jaxpr/ppermute | solution.py:18
  44.9 11.1 %collective-permute-start = (bf16[64,2,4,128]{3,0,2,1:T(8,128)(2,1)}, bf16[64,2,4,128]{3,0,2,1:T(8,128)(2,1)S(1)}, u32[]{:S(2)}, u32[]{:S(2)}) collective-permute-start(bf16[64,2,4,128]{3,0,2,1:T(8,128)(2,1)} %broadcast_select_fusion.4), channel_id=1, source_target_pairs={{0,32},{32,64},{64,96},{96,128},{128,160},{160,192},{192,224},{224... | collective-permute-start | bytes 393224 | tf_op jit(solution)/shard_map/while/body/eval_jaxpr/ppermute | solution.py:26
  46.8 10.5 %collective-permute-start.1 = (bf16[64,2,4,128]{3,0,2,1:T(8,128)(2,1)S(1)}, bf16[64,2,4,128]{3,0,2,1:T(8,128)(2,1)S(1)}, u32[]{:S(2)}, u32[]{:S(2)}) collective-permute-start(bf16[64,2,4,128]{3,0,2,1:T(8,128)(2,1)S(1)} %broadcast_select_fusion.5), channel_id=1, source_target_pairs={{32,0},{64,32},{96,64},{128,96},{160,128},{192,160},{224,192},{256... | collective-permute-start | bytes 393224 | tf_op jit(solution)/shard_map/while/body/eval_jaxpr/ppermute | solution.py:26
  59.9 8.1 %collective-permute-start.3 = (bf16[128,1,4,128]{3,0,2,1:T(8,128)(2,1)S(1)}, bf16[128,1,4,128]{3,0,2,1:T(8,128)(2,1)S(1)}, u32[]{:S(2)}, u32[]{:S(2)}) collective-permute-start(bf16[128,1,4,128]{3,0,2,1:T(8,128)(2,1)S(1)} %get-tuple-element.364), channel_id=1, source_target_pairs={{0,4},{4,8},{8,12},{12,16},{16,20},{20,24},{24,28},{1,5},{5,9},{9,... | collective-permute-start | bytes 393224 | tf_op jit(solution)/shard_map/while/body/eval_jaxpr/ppermute | solution.py:17
  68.0 8.7 %collective-permute-start.4 = (bf16[128,4,1,128]{3,0,2,1:T(8,128)(2,1)S(1)}, bf16[128,4,1,128]{3,0,2,1:T(8,128)(2,1)S(1)}, u32[]{:S(2)}, u32[]{:S(2)}) collective-permute-start(bf16[128,4,1,128]{3,0,2,1:T(8,128)(2,1)S(1)} %get-tuple-element.365), channel_id=1, source_target_pairs={{1,0},{2,1},{3,2},{5,4},{6,5},{7,6},{9,8},{10,9},{11,10},{13,12},{... | collective-permute-start | bytes 393224 | tf_op jit(solution)/shard_map/while/body/eval_jaxpr/ppermute | solution.py:18
  78.5 11.1 %collective-permute-start = (bf16[64,2,4,128]{3,0,2,1:T(8,128)(2,1)}, bf16[64,2,4,128]{3,0,2,1:T(8,128)(2,1)S(1)}, u32[]{:S(2)}, u32[]{:S(2)}) collective-permute-start(bf16[64,2,4,128]{3,0,2,1:T(8,128)(2,1)} %broadcast_select_fusion.4), channel_id=1, source_target_pairs={{0,32},{32,64},{64,96},{96,128},{128,160},{160,192},{192,224},{224... | collective-permute-start | bytes 393224 | tf_op jit(solution)/shard_map/while/body/eval_jaxpr/ppermute | solution.py:26
  80.5 10.5 %collective-permute-start.1 = (bf16[64,2,4,128]{3,0,2,1:T(8,128)(2,1)S(1)}, bf16[64,2,4,128]{3,0,2,1:T(8,128)(2,1)S(1)}, u32[]{:S(2)}, u32[]{:S(2)}) collective-permute-start(bf16[64,2,4,128]{3,0,2,1:T(8,128)(2,1)S(1)} %broadcast_select_fusion.5), channel_id=1, source_target_pairs={{32,0},{64,32},{96,64},{128,96},{160,128},{192,160},{224,192},{256... | collective-permute-start | bytes 393224 | tf_op jit(solution)/shard_map/while/body/eval_jaxpr/ppermute | solution.py:26
  93.6 8.1 %collective-permute-start.3 = (bf16[128,1,4,128]{3,0,2,1:T(8,128)(2,1)S(1)}, bf16[128,1,4,128]{3,0,2,1:T(8,128)(2,1)S(1)}, u32[]{:S(2)}, u32[]{:S(2)}) collective-permute-start(bf16[128,1,4,128]{3,0,2,1:T(8,128)(2,1)S(1)} %get-tuple-element.364), channel_id=1, source_target_pairs={{0,4},{4,8},{8,12},{12,16},{16,20},{20,24},{24,28},{1,5},{5,9},{9,... | collective-permute-start | bytes 393224 | tf_op jit(solution)/shard_map/while/body/eval_jaxpr/ppermute | solution.py:17
  101.7 8.7 %collective-permute-start.4 = (bf16[128,4,1,128]{3,0,2,1:T(8,128)(2,1)S(1)}, bf16[128,4,1,128]{3,0,2,1:T(8,128)(2,1)S(1)}, u32[]{:S(2)}, u32[]{:S(2)}) collective-permute-start(bf16[128,4,1,128]{3,0,2,1:T(8,128)(2,1)S(1)} %get-tuple-element.365), channel_id=1, source_target_pairs={{1,0},{2,1},{3,2},{5,4},{6,5},{7,6},{9,8},{10,9},{11,10},{13,12},{... | collective-permute-start | bytes 393224 | tf_op jit(solution)/shard_map/while/body/eval_jaxpr/ppermute | solution.py:18
  112.1 11.1 %collective-permute-start = (bf16[64,2,4,128]{3,0,2,1:T(8,128)(2,1)}, bf16[64,2,4,128]{3,0,2,1:T(8,128)(2,1)S(1)}, u32[]{:S(2)}, u32[]{:S(2)}) collective-permute-start(bf16[64,2,4,128]{3,0,2,1:T(8,128)(2,1)} %broadcast_select_fusion.4), channel_id=1, source_target_pairs={{0,32},{32,64},{64,96},{96,128},{128,160},{160,192},{192,224},{224... | collective-permute-start | bytes 393224 | tf_op jit(solution)/shard_map/while/body/eval_jaxpr/ppermute | solution.py:26
  114.1 10.5 %collective-permute-start.1 = (bf16[64,2,4,128]{3,0,2,1:T(8,128)(2,1)S(1)}, bf16[64,2,4,128]{3,0,2,1:T(8,128)(2,1)S(1)}, u32[]{:S(2)}, u32[]{:S(2)}) collective-permute-start(bf16[64,2,4,128]{3,0,2,1:T(8,128)(2,1)S(1)} %broadcast_select_fusion.5), channel_id=1, source_target_pairs={{32,0},{64,32},{96,64},{128,96},{160,128},{192,160},{224,192},{256... | collective-permute-start | bytes 393224 | tf_op jit(solution)/shard_map/while/body/eval_jaxpr/ppermute | solution.py:26
  127.2 8.1 %collective-permute-start.3 = (bf16[128,1,4,128]{3,0,2,1:T(8,128)(2,1)S(1)}, bf16[128,1,4,128]{3,0,2,1:T(8,128)(2,1)S(1)}, u32[]{:S(2)}, u32[]{:S(2)}) collective-permute-start(bf16[128,1,4,128]{3,0,2,1:T(8,128)(2,1)S(1)} %get-tuple-element.364), channel_id=1, source_target_pairs={{0,4},{4,8},{8,12},{12,16},{16,20},{20,24},{24,28},{1,5},{5,9},{9,... | collective-permute-start | bytes 393224 | tf_op jit(solution)/shard_map/while/body/eval_jaxpr/ppermute | solution.py:17
  135.3 8.7 %collective-permute-start.4 = (bf16[128,4,1,128]{3,0,2,1:T(8,128)(2,1)S(1)}, bf16[128,4,1,128]{3,0,2,1:T(8,128)(2,1)S(1)}, u32[]{:S(2)}, u32[]{:S(2)}) collective-permute-start(bf16[128,4,1,128]{3,0,2,1:T(8,128)(2,1)S(1)} %get-tuple-element.365), channel_id=1, source_target_pairs={{1,0},{2,1},{3,2},{5,4},{6,5},{7,6},{9,8},{10,9},{11,10},{13,12},{... | collective-permute-start | bytes 393224 | tf_op jit(solution)/shard_map/while/body/eval_jaxpr/ppermute | solution.py:18
  145.8 11.1 %collective-permute-start = (bf16[64,2,4,128]{3,0,2,1:T(8,128)(2,1)}, bf16[64,2,4,128]{3,0,2,1:T(8,128)(2,1)S(1)}, u32[]{:S(2)}, u32[]{:S(2)}) collective-permute-start(bf16[64,2,4,128]{3,0,2,1:T(8,128)(2,1)} %broadcast_select_fusion.4), channel_id=1, source_target_pairs={{0,32},{32,64},{64,96},{96,128},{128,160},{160,192},{192,224},{224... | collective-permute-start | bytes 393224 | tf_op jit(solution)/shard_map/while/body/eval_jaxpr/ppermute | solution.py:26
  147.7 10.5 %collective-permute-start.1 = (bf16[64,2,4,128]{3,0,2,1:T(8,128)(2,1)S(1)}, bf16[64,2,4,128]{3,0,2,1:T(8,128)(2,1)S(1)}, u32[]{:S(2)}, u32[]{:S(2)}) collective-permute-start(bf16[64,2,4,128]{3,0,2,1:T(8,128)(2,1)S(1)} %broadcast_select_fusion.5), channel_id=1, source_target_pairs={{32,0},{64,32},{96,64},{128,96},{160,128},{192,160},{224,192},{256... | collective-permute-start | bytes 393224 | tf_op jit(solution)/shard_map/while/body/eval_jaxpr/ppermute | solution.py:26
  160.8 8.1 %collective-permute-start.3 = (bf16[128,1,4,128]{3,0,2,1:T(8,128)(2,1)S(1)}, bf16[128,1,4,128]{3,0,2,1:T(8,128)(2,1)S(1)}, u32[]{:S(2)}, u32[]{:S(2)}) collective-permute-start(bf16[128,1,4,128]{3,0,2,1:T(8,128)(2,1)S(1)} %get-tuple-element.364), channel_id=1, source_target_pairs={{0,4},{4,8},{8,12},{12,16},{16,20},{20,24},{24,28},{1,5},{5,9},{9,... | collective-permute-start | bytes 393224 | tf_op jit(solution)/shard_map/while/body/eval_jaxpr/ppermute | solution.py:17
  168.9 8.7 %collective-permute-start.4 = (bf16[128,4,1,128]{3,0,2,1:T(8,128)(2,1)S(1)}, bf16[128,4,1,128]{3,0,2,1:T(8,128)(2,1)S(1)}, u32[]{:S(2)}, u32[]{:S(2)}) collective-permute-start(bf16[128,4,1,128]{3,0,2,1:T(8,128)(2,1)S(1)} %get-tuple-element.365), channel_id=1, source_target_pairs={{1,0},{2,1},{3,2},{5,4},{6,5},{7,6},{9,8},{10,9},{11,10},{13,12},{... | collective-permute-start | bytes 393224 | tf_op jit(solution)/shard_map/while/body/eval_jaxpr/ppermute | solution.py:18
  179.4 11.2 %collective-permute-start = (bf16[64,2,4,128]{3,0,2,1:T(8,128)(2,1)}, bf16[64,2,4,128]{3,0,2,1:T(8,128)(2,1)S(1)}, u32[]{:S(2)}, u32[]{:S(2)}) collective-permute-start(bf16[64,2,4,128]{3,0,2,1:T(8,128)(2,1)} %broadcast_select_fusion.4), channel_id=1, source_target_pairs={{0,32},{32,64},{64,96},{96,128},{128,160},{160,192},{192,224},{224... | collective-permute-start | bytes 393224 | tf_op jit(solution)/shard_map/while/body/eval_jaxpr/ppermute | solution.py:26
  181.3 10.6 %collective-permute-start.1 = (bf16[64,2,4,128]{3,0,2,1:T(8,128)(2,1)S(1)}, bf16[64,2,4,128]{3,0,2,1:T(8,128)(2,1)S(1)}, u32[]{:S(2)}, u32[]{:S(2)}) collective-permute-start(bf16[64,2,4,128]{3,0,2,1:T(8,128)(2,1)S(1)} %broadcast_select_fusion.5), channel_id=1, source_target_pairs={{32,0},{64,32},{96,64},{128,96},{160,128},{192,160},{224,192},{256... | collective-permute-start | bytes 393224 | tf_op jit(solution)/shard_map/while/body/eval_jaxpr/ppermute | solution.py:26
  194.5 8.1 %collective-permute-start.3 = (bf16[128,1,4,128]{3,0,2,1:T(8,128)(2,1)S(1)}, bf16[128,1,4,128]{3,0,2,1:T(8,128)(2,1)S(1)}, u32[]{:S(2)}, u32[]{:S(2)}) collective-permute-start(bf16[128,1,4,128]{3,0,2,1:T(8,128)(2,1)S(1)} %get-tuple-element.364), channel_id=1, source_target_pairs={{0,4},{4,8},{8,12},{12,16},{16,20},{20,24},{24,28},{1,5},{5,9},{9,... | collective-permute-start | bytes 393224 | tf_op jit(solution)/shard_map/while/body/eval_jaxpr/ppermute | solution.py:17
  202.6 8.7 %collective-permute-start.4 = (bf16[128,4,1,128]{3,0,2,1:T(8,128)(2,1)S(1)}, bf16[128,4,1,128]{3,0,2,1:T(8,128)(2,1)S(1)}, u32[]{:S(2)}, u32[]{:S(2)}) collective-permute-start(bf16[128,4,1,128]{3,0,2,1:T(8,128)(2,1)S(1)} %get-tuple-element.365), channel_id=1, source_target_pairs={{1,0},{2,1},{3,2},{5,4},{6,5},{7,6},{9,8},{10,9},{11,10},{13,12},{... | collective-permute-start | bytes 393224 | tf_op jit(solution)/shard_map/while/body/eval_jaxpr/ppermute | solution.py:18
  213.1 11.1 %collective-permute-start = (bf16[64,2,4,128]{3,0,2,1:T(8,128)(2,1)}, bf16[64,2,4,128]{3,0,2,1:T(8,128)(2,1)S(1)}, u32[]{:S(2)}, u32[]{:S(2)}) collective-permute-start(bf16[64,2,4,128]{3,0,2,1:T(8,128)(2,1)} %broadcast_select_fusion.4), channel_id=1, source_target_pairs={{0,32},{32,64},{64,96},{96,128},{128,160},{160,192},{192,224},{224... | collective-permute-start | bytes 393224 | tf_op jit(solution)/shard_map/while/body/eval_jaxpr/ppermute | solution.py:26
  215.1 10.5 %collective-permute-start.1 = (bf16[64,2,4,128]{3,0,2,1:T(8,128)(2,1)S(1)}, bf16[64,2,4,128]{3,0,2,1:T(8,128)(2,1)S(1)}, u32[]{:S(2)}, u32[]{:S(2)}) collective-permute-start(bf16[64,2,4,128]{3,0,2,1:T(8,128)(2,1)S(1)} %broadcast_select_fusion.5), channel_id=1, source_target_pairs={{32,0},{64,32},{96,64},{128,96},{160,128},{192,160},{224,192},{256... | collective-permute-start | bytes 393224 | tf_op jit(solution)/shard_map/while/body/eval_jaxpr/ppermute | solution.py:26
  228.2 8.1 %collective-permute-start.3 = (bf16[128,1,4,128]{3,0,2,1:T(8,128)(2,1)S(1)}, bf16[128,1,4,128]{3,0,2,1:T(8,128)(2,1)S(1)}, u32[]{:S(2)}, u32[]{:S(2)}) collective-permute-start(bf16[128,1,4,128]{3,0,2,1:T(8,128)(2,1)S(1)} %get-tuple-element.364), channel_id=1, source_target_pairs={{0,4},{4,8},{8,12},{12,16},{16,20},{20,24},{24,28},{1,5},{5,9},{9,... | collective-permute-start | bytes 393224 | tf_op jit(solution)/shard_map/while/body/eval_jaxpr/ppermute | solution.py:17
  236.3 8.7 %collective-permute-start.4 = (bf16[128,4,1,128]{3,0,2,1:T(8,128)(2,1)S(1)}, bf16[128,4,1,128]{3,0,2,1:T(8,128)(2,1)S(1)}, u32[]{:S(2)}, u32[]{:S(2)}) collective-permute-start(bf16[128,4,1,128]{3,0,2,1:T(8,128)(2,1)S(1)} %get-tuple-element.365), channel_id=1, source_target_pairs={{1,0},{2,1},{3,2},{5,4},{6,5},{7,6},{9,8},{10,9},{11,10},{13,12},{... | collective-permute-start | bytes 393224 | tf_op jit(solution)/shard_map/while/body/eval_jaxpr/ppermute | solution.py:18
  246.7 11.1 %collective-permute-start = (bf16[64,2,4,128]{3,0,2,1:T(8,128)(2,1)}, bf16[64,2,4,128]{3,0,2,1:T(8,128)(2,1)S(1)}, u32[]{:S(2)}, u32[]{:S(2)}) collective-permute-start(bf16[64,2,4,128]{3,0,2,1:T(8,128)(2,1)} %broadcast_select_fusion.4), channel_id=1, source_target_pairs={{0,32},{32,64},{64,96},{96,128},{128,160},{160,192},{192,224},{224... | collective-permute-start | bytes 393224 | tf_op jit(solution)/shard_map/while/body/eval_jaxpr/ppermute | solution.py:26
  248.7 10.5 %collective-permute-start.1 = (bf16[64,2,4,128]{3,0,2,1:T(8,128)(2,1)S(1)}, bf16[64,2,4,128]{3,0,2,1:T(8,128)(2,1)S(1)}, u32[]{:S(2)}, u32[]{:S(2)}) collective-permute-start(bf16[64,2,4,128]{3,0,2,1:T(8,128)(2,1)S(1)} %broadcast_select_fusion.5), channel_id=1, source_target_pairs={{32,0},{64,32},{96,64},{128,96},{160,128},{192,160},{224,192},{256... | collective-permute-start | bytes 393224 | tf_op jit(solution)/shard_map/while/body/eval_jaxpr/ppermute | solution.py:26
  261.8 8.1 %collective-permute-start.3 = (bf16[128,1,4,128]{3,0,2,1:T(8,128)(2,1)S(1)}, bf16[128,1,4,128]{3,0,2,1:T(8,128)(2,1)S(1)}, u32[]{:S(2)}, u32[]{:S(2)}) collective-permute-start(bf16[128,1,4,128]{3,0,2,1:T(8,128)(2,1)S(1)} %get-tuple-element.364), channel_id=1, source_target_pairs={{0,4},{4,8},{8,12},{12,16},{16,20},{20,24},{24,28},{1,5},{5,9},{9,... | collective-permute-start | bytes 393224 | tf_op jit(solution)/shard_map/while/body/eval_jaxpr/ppermute | solution.py:17
  269.9 8.7 %collective-permute-start.4 = (bf16[128,4,1,128]{3,0,2,1:T(8,128)(2,1)S(1)}, bf16[128,4,1,128]{3,0,2,1:T(8,128)(2,1)S(1)}, u32[]{:S(2)}, u32[]{:S(2)}) collective-permute-start(bf16[128,4,1,128]{3,0,2,1:T(8,128)(2,1)S(1)} %get-tuple-element.365), channel_id=1, source_target_pairs={{1,0},{2,1},{3,2},{5,4},{6,5},{7,6},{9,8},{10,9},{11,10},{13,12},{... | collective-permute-start | bytes 393224 | tf_op jit(solution)/shard_map/while/body/eval_jaxpr/ppermute | solution.py:18
  280.4 11.1 %collective-permute-start = (bf16[64,2,4,128]{3,0,2,1:T(8,128)(2,1)}, bf16[64,2,4,128]{3,0,2,1:T(8,128)(2,1)S(1)}, u32[]{:S(2)}, u32[]{:S(2)}) collective-permute-start(bf16[64,2,4,128]{3,0,2,1:T(8,128)(2,1)} %broadcast_select_fusion.4), channel_id=1, source_target_pairs={{0,32},{32,64},{64,96},{96,128},{128,160},{160,192},{192,224},{224... | collective-permute-start | bytes 393224 | tf_op jit(solution)/shard_map/while/body/eval_jaxpr/ppermute | solution.py:26
  282.3 10.5 %collective-permute-start.1 = (bf16[64,2,4,128]{3,0,2,1:T(8,128)(2,1)S(1)}, bf16[64,2,4,128]{3,0,2,1:T(8,128)(2,1)S(1)}, u32[]{:S(2)}, u32[]{:S(2)}) collective-permute-start(bf16[64,2,4,128]{3,0,2,1:T(8,128)(2,1)S(1)} %broadcast_select_fusion.5), channel_id=1, source_target_pairs={{32,0},{64,32},{96,64},{128,96},{160,128},{192,160},{224,192},{256... | collective-permute-start | bytes 393224 | tf_op jit(solution)/shard_map/while/body/eval_jaxpr/ppermute | solution.py:26
  295.4 8.1 %collective-permute-start.3 = (bf16[128,1,4,128]{3,0,2,1:T(8,128)(2,1)S(1)}, bf16[128,1,4,128]{3,0,2,1:T(8,128)(2,1)S(1)}, u32[]{:S(2)}, u32[]{:S(2)}) collective-permute-start(bf16[128,1,4,128]{3,0,2,1:T(8,128)(2,1)S(1)} %get-tuple-element.364), channel_id=1, source_target_pairs={{0,4},{4,8},{8,12},{12,16},{16,20},{20,24},{24,28},{1,5},{5,9},{9,... | collective-permute-start | bytes 393224 | tf_op jit(solution)/shard_map/while/body/eval_jaxpr/ppermute | solution.py:17
  303.5 8.7 %collective-permute-start.4 = (bf16[128,4,1,128]{3,0,2,1:T(8,128)(2,1)S(1)}, bf16[128,4,1,128]{3,0,2,1:T(8,128)(2,1)S(1)}, u32[]{:S(2)}, u32[]{:S(2)}) collective-permute-start(bf16[128,4,1,128]{3,0,2,1:T(8,128)(2,1)S(1)} %get-tuple-element.365), channel_id=1, source_target_pairs={{1,0},{2,1},{3,2},{5,4},{6,5},{7,6},{9,8},{10,9},{11,10},{13,12},{... | collective-permute-start | bytes 393224 | tf_op jit(solution)/shard_map/while/body/eval_jaxpr/ppermute | solution.py:18
  314.0 11.1 %collective-permute-start = (bf16[64,2,4,128]{3,0,2,1:T(8,128)(2,1)}, bf16[64,2,4,128]{3,0,2,1:T(8,128)(2,1)S(1)}, u32[]{:S(2)}, u32[]{:S(2)}) collective-permute-start(bf16[64,2,4,128]{3,0,2,1:T(8,128)(2,1)} %broadcast_select_fusion.4), channel_id=1, source_target_pairs={{0,32},{32,64},{64,96},{96,128},{128,160},{160,192},{192,224},{224... | collective-permute-start | bytes 393224 | tf_op jit(solution)/shard_map/while/body/eval_jaxpr/ppermute | solution.py:26
  315.9 10.5 %collective-permute-start.1 = (bf16[64,2,4,128]{3,0,2,1:T(8,128)(2,1)S(1)}, bf16[64,2,4,128]{3,0,2,1:T(8,128)(2,1)S(1)}, u32[]{:S(2)}, u32[]{:S(2)}) collective-permute-start(bf16[64,2,4,128]{3,0,2,1:T(8,128)(2,1)S(1)} %broadcast_select_fusion.5), channel_id=1, source_target_pairs={{32,0},{64,32},{96,64},{128,96},{160,128},{192,160},{224,192},{256... | collective-permute-start | bytes 393224 | tf_op jit(solution)/shard_map/while/body/eval_jaxpr/ppermute | solution.py:26
  329.0 8.1 %collective-permute-start.3 = (bf16[128,1,4,128]{3,0,2,1:T(8,128)(2,1)S(1)}, bf16[128,1,4,128]{3,0,2,1:T(8,128)(2,1)S(1)}, u32[]{:S(2)}, u32[]{:S(2)}) collective-permute-start(bf16[128,1,4,128]{3,0,2,1:T(8,128)(2,1)S(1)} %get-tuple-element.364), channel_id=1, source_target_pairs={{0,4},{4,8},{8,12},{12,16},{16,20},{20,24},{24,28},{1,5},{5,9},{9,... | collective-permute-start | bytes 393224 | tf_op jit(solution)/shard_map/while/body/eval_jaxpr/ppermute | solution.py:17
  337.1 8.7 %collective-permute-start.4 = (bf16[128,4,1,128]{3,0,2,1:T(8,128)(2,1)S(1)}, bf16[128,4,1,128]{3,0,2,1:T(8,128)(2,1)S(1)}, u32[]{:S(2)}, u32[]{:S(2)}) collective-permute-start(bf16[128,4,1,128]{3,0,2,1:T(8,128)(2,1)S(1)} %get-tuple-element.365), channel_id=1, source_target_pairs={{1,0},{2,1},{3,2},{5,4},{6,5},{7,6},{9,8},{10,9},{11,10},{13,12},{... | collective-permute-start | bytes 393224 | tf_op jit(solution)/shard_map/while/body/eval_jaxpr/ppermute | solution.py:18
  347.6 11.1 %collective-permute-start = (bf16[64,2,4,128]{3,0,2,1:T(8,128)(2,1)}, bf16[64,2,4,128]{3,0,2,1:T(8,128)(2,1)S(1)}, u32[]{:S(2)}, u32[]{:S(2)}) collective-permute-start(bf16[64,2,4,128]{3,0,2,1:T(8,128)(2,1)} %broadcast_select_fusion.4), channel_id=1, source_target_pairs={{0,32},{32,64},{64,96},{96,128},{128,160},{160,192},{192,224},{224... | collective-permute-start | bytes 393224 | tf_op jit(solution)/shard_map/while/body/eval_jaxpr/ppermute | solution.py:26
  349.6 10.5 %collective-permute-start.1 = (bf16[64,2,4,128]{3,0,2,1:T(8,128)(2,1)S(1)}, bf16[64,2,4,128]{3,0,2,1:T(8,128)(2,1)S(1)}, u32[]{:S(2)}, u32[]{:S(2)}) collective-permute-start(bf16[64,2,4,128]{3,0,2,1:T(8,128)(2,1)S(1)} %broadcast_select_fusion.5), channel_id=1, source_target_pairs={{32,0},{64,32},{96,64},{128,96},{160,128},{192,160},{224,192},{256... | collective-permute-start | bytes 393224 | tf_op jit(solution)/shard_map/while/body/eval_jaxpr/ppermute | solution.py:26
  362.7 8.1 %collective-permute-start.3 = (bf16[128,1,4,128]{3,0,2,1:T(8,128)(2,1)S(1)}, bf16[128,1,4,128]{3,0,2,1:T(8,128)(2,1)S(1)}, u32[]{:S(2)}, u32[]{:S(2)}) collective-permute-start(bf16[128,1,4,128]{3,0,2,1:T(8,128)(2,1)S(1)} %get-tuple-element.364), channel_id=1, source_target_pairs={{0,4},{4,8},{8,12},{12,16},{16,20},{20,24},{24,28},{1,5},{5,9},{9,... | collective-permute-start | bytes 393224 | tf_op jit(solution)/shard_map/while/body/eval_jaxpr/ppermute | solution.py:17
  370.8 8.7 %collective-permute-start.4 = (bf16[128,4,1,128]{3,0,2,1:T(8,128)(2,1)S(1)}, bf16[128,4,1,128]{3,0,2,1:T(8,128)(2,1)S(1)}, u32[]{:S(2)}, u32[]{:S(2)}) collective-permute-start(bf16[128,4,1,128]{3,0,2,1:T(8,128)(2,1)S(1)} %get-tuple-element.365), channel_id=1, source_target_pairs={{1,0},{2,1},{3,2},{5,4},{6,5},{7,6},{9,8},{10,9},{11,10},{13,12},{... | collective-permute-start | bytes 393224 | tf_op jit(solution)/shard_map/while/body/eval_jaxpr/ppermute | solution.py:18
  381.2 11.1 %collective-permute-start = (bf16[64,2,4,128]{3,0,2,1:T(8,128)(2,1)}, bf16[64,2,4,128]{3,0,2,1:T(8,128)(2,1)S(1)}, u32[]{:S(2)}, u32[]{:S(2)}) collective-permute-start(bf16[64,2,4,128]{3,0,2,1:T(8,128)(2,1)} %broadcast_select_fusion.4), channel_id=1, source_target_pairs={{0,32},{32,64},{64,96},{96,128},{128,160},{160,192},{192,224},{224... | collective-permute-start | bytes 393224 | tf_op jit(solution)/shard_map/while/body/eval_jaxpr/ppermute | solution.py:26
  383.2 10.5 %collective-permute-start.1 = (bf16[64,2,4,128]{3,0,2,1:T(8,128)(2,1)S(1)}, bf16[64,2,4,128]{3,0,2,1:T(8,128)(2,1)S(1)}, u32[]{:S(2)}, u32[]{:S(2)}) collective-permute-start(bf16[64,2,4,128]{3,0,2,1:T(8,128)(2,1)S(1)} %broadcast_select_fusion.5), channel_id=1, source_target_pairs={{32,0},{64,32},{96,64},{128,96},{160,128},{192,160},{224,192},{256... | collective-permute-start | bytes 393224 | tf_op jit(solution)/shard_map/while/body/eval_jaxpr/ppermute | solution.py:26
  396.3 8.1 %collective-permute-start.3 = (bf16[128,1,4,128]{3,0,2,1:T(8,128)(2,1)S(1)}, bf16[128,1,4,128]{3,0,2,1:T(8,128)(2,1)S(1)}, u32[]{:S(2)}, u32[]{:S(2)}) collective-permute-start(bf16[128,1,4,128]{3,0,2,1:T(8,128)(2,1)S(1)} %get-tuple-element.364), channel_id=1, source_target_pairs={{0,4},{4,8},{8,12},{12,16},{16,20},{20,24},{24,28},{1,5},{5,9},{9,... | collective-permute-start | bytes 393224 | tf_op jit(solution)/shard_map/while/body/eval_jaxpr/ppermute | solution.py:17
  404.4 8.7 %collective-permute-start.4 = (bf16[128,4,1,128]{3,0,2,1:T(8,128)(2,1)S(1)}, bf16[128,4,1,128]{3,0,2,1:T(8,128)(2,1)S(1)}, u32[]{:S(2)}, u32[]{:S(2)}) collective-permute-start(bf16[128,4,1,128]{3,0,2,1:T(8,128)(2,1)S(1)} %get-tuple-element.365), channel_id=1, source_target_pairs={{1,0},{2,1},{3,2},{5,4},{6,5},{7,6},{9,8},{10,9},{11,10},{13,12},{... | collective-permute-start | bytes 393224 | tf_op jit(solution)/shard_map/while/body/eval_jaxpr/ppermute | solution.py:18
  414.9 11.1 %collective-permute-start = (bf16[64,2,4,128]{3,0,2,1:T(8,128)(2,1)}, bf16[64,2,4,128]{3,0,2,1:T(8,128)(2,1)S(1)}, u32[]{:S(2)}, u32[]{:S(2)}) collective-permute-start(bf16[64,2,4,128]{3,0,2,1:T(8,128)(2,1)} %broadcast_select_fusion.4), channel_id=1, source_target_pairs={{0,32},{32,64},{64,96},{96,128},{128,160},{160,192},{192,224},{224... | collective-permute-start | bytes 393224 | tf_op jit(solution)/shard_map/while/body/eval_jaxpr/ppermute | solution.py:26
  416.8 10.5 %collective-permute-start.1 = (bf16[64,2,4,128]{3,0,2,1:T(8,128)(2,1)S(1)}, bf16[64,2,4,128]{3,0,2,1:T(8,128)(2,1)S(1)}, u32[]{:S(2)}, u32[]{:S(2)}) collective-permute-start(bf16[64,2,4,128]{3,0,2,1:T(8,128)(2,1)S(1)} %broadcast_select_fusion.5), channel_id=1, source_target_pairs={{32,0},{64,32},{96,64},{128,96},{160,128},{192,160},{224,192},{256... | collective-permute-start | bytes 393224 | tf_op jit(solution)/shard_map/while/body/eval_jaxpr/ppermute | solution.py:26
  429.9 8.1 %collective-permute-start.3 = (bf16[128,1,4,128]{3,0,2,1:T(8,128)(2,1)S(1)}, bf16[128,1,4,128]{3,0,2,1:T(8,128)(2,1)S(1)}, u32[]{:S(2)}, u32[]{:S(2)}) collective-permute-start(bf16[128,1,4,128]{3,0,2,1:T(8,128)(2,1)S(1)} %get-tuple-element.364), channel_id=1, source_target_pairs={{0,4},{4,8},{8,12},{12,16},{16,20},{20,24},{24,28},{1,5},{5,9},{9,... | collective-permute-start | bytes 393224 | tf_op jit(solution)/shard_map/while/body/eval_jaxpr/ppermute | solution.py:17
  438.0 8.7 %collective-permute-start.4 = (bf16[128,4,1,128]{3,0,2,1:T(8,128)(2,1)S(1)}, bf16[128,4,1,128]{3,0,2,1:T(8,128)(2,1)S(1)}, u32[]{:S(2)}, u32[]{:S(2)}) collective-permute-start(bf16[128,4,1,128]{3,0,2,1:T(8,128)(2,1)S(1)} %get-tuple-element.365), channel_id=1, source_target_pairs={{1,0},{2,1},{3,2},{5,4},{6,5},{7,6},{9,8},{10,9},{11,10},{13,12},{... | collective-permute-start | bytes 393224 | tf_op jit(solution)/shard_map/while/body/eval_jaxpr/ppermute | solution.py:18
  448.5 11.1 %collective-permute-start = (bf16[64,2,4,128]{3,0,2,1:T(8,128)(2,1)}, bf16[64,2,4,128]{3,0,2,1:T(8,128)(2,1)S(1)}, u32[]{:S(2)}, u32[]{:S(2)}) collective-permute-start(bf16[64,2,4,128]{3,0,2,1:T(8,128)(2,1)} %broadcast_select_fusion.4), channel_id=1, source_target_pairs={{0,32},{32,64},{64,96},{96,128},{128,160},{160,192},{192,224},{224... | collective-permute-start | bytes 393224 | tf_op jit(solution)/shard_map/while/body/eval_jaxpr/ppermute | solution.py:26
  450.4 10.5 %collective-permute-start.1 = (bf16[64,2,4,128]{3,0,2,1:T(8,128)(2,1)S(1)}, bf16[64,2,4,128]{3,0,2,1:T(8,128)(2,1)S(1)}, u32[]{:S(2)}, u32[]{:S(2)}) collective-permute-start(bf16[64,2,4,128]{3,0,2,1:T(8,128)(2,1)S(1)} %broadcast_select_fusion.5), channel_id=1, source_target_pairs={{32,0},{64,32},{96,64},{128,96},{160,128},{192,160},{224,192},{256... | collective-permute-start | bytes 393224 | tf_op jit(solution)/shard_map/while/body/eval_jaxpr/ppermute | solution.py:26
  463.5 8.1 %collective-permute-start.3 = (bf16[128,1,4,128]{3,0,2,1:T(8,128)(2,1)S(1)}, bf16[128,1,4,128]{3,0,2,1:T(8,128)(2,1)S(1)}, u32[]{:S(2)}, u32[]{:S(2)}) collective-permute-start(bf16[128,1,4,128]{3,0,2,1:T(8,128)(2,1)S(1)} %get-tuple-element.364), channel_id=1, source_target_pairs={{0,4},{4,8},{8,12},{12,16},{16,20},{20,24},{24,28},{1,5},{5,9},{9,... | collective-permute-start | bytes 393224 | tf_op jit(solution)/shard_map/while/body/eval_jaxpr/ppermute | solution.py:17
  471.6 8.7 %collective-permute-start.4 = (bf16[128,4,1,128]{3,0,2,1:T(8,128)(2,1)S(1)}, bf16[128,4,1,128]{3,0,2,1:T(8,128)(2,1)S(1)}, u32[]{:S(2)}, u32[]{:S(2)}) collective-permute-start(bf16[128,4,1,128]{3,0,2,1:T(8,128)(2,1)S(1)} %get-tuple-element.365), channel_id=1, source_target_pairs={{1,0},{2,1},{3,2},{5,4},{6,5},{7,6},{9,8},{10,9},{11,10},{13,12},{... | collective-permute-start | bytes 393224 | tf_op jit(solution)/shard_map/while/body/eval_jaxpr/ppermute | solution.py:18
  482.1 11.1 %collective-permute-start = (bf16[64,2,4,128]{3,0,2,1:T(8,128)(2,1)}, bf16[64,2,4,128]{3,0,2,1:T(8,128)(2,1)S(1)}, u32[]{:S(2)}, u32[]{:S(2)}) collective-permute-start(bf16[64,2,4,128]{3,0,2,1:T(8,128)(2,1)} %broadcast_select_fusion.4), channel_id=1, source_target_pairs={{0,32},{32,64},{64,96},{96,128},{128,160},{160,192},{192,224},{224... | collective-permute-start | bytes 393224 | tf_op jit(solution)/shard_map/while/body/eval_jaxpr/ppermute | solution.py:26
  484.1 10.5 %collective-permute-start.1 = (bf16[64,2,4,128]{3,0,2,1:T(8,128)(2,1)S(1)}, bf16[64,2,4,128]{3,0,2,1:T(8,128)(2,1)S(1)}, u32[]{:S(2)}, u32[]{:S(2)}) collective-permute-start(bf16[64,2,4,128]{3,0,2,1:T(8,128)(2,1)S(1)} %broadcast_select_fusion.5), channel_id=1, source_target_pairs={{32,0},{64,32},{96,64},{128,96},{160,128},{192,160},{224,192},{256... | collective-permute-start | bytes 393224 | tf_op jit(solution)/shard_map/while/body/eval_jaxpr/ppermute | solution.py:26
  497.2 8.1 %collective-permute-start.3 = (bf16[128,1,4,128]{3,0,2,1:T(8,128)(2,1)S(1)}, bf16[128,1,4,128]{3,0,2,1:T(8,128)(2,1)S(1)}, u32[]{:S(2)}, u32[]{:S(2)}) collective-permute-start(bf16[128,1,4,128]{3,0,2,1:T(8,128)(2,1)S(1)} %get-tuple-element.364), channel_id=1, source_target_pairs={{0,4},{4,8},{8,12},{12,16},{16,20},{20,24},{24,28},{1,5},{5,9},{9,... | collective-permute-start | bytes 393224 | tf_op jit(solution)/shard_map/while/body/eval_jaxpr/ppermute | solution.py:17
  505.3 8.7 %collective-permute-start.4 = (bf16[128,4,1,128]{3,0,2,1:T(8,128)(2,1)S(1)}, bf16[128,4,1,128]{3,0,2,1:T(8,128)(2,1)S(1)}, u32[]{:S(2)}, u32[]{:S(2)}) collective-permute-start(bf16[128,4,1,128]{3,0,2,1:T(8,128)(2,1)S(1)} %get-tuple-element.365), channel_id=1, source_target_pairs={{1,0},{2,1},{3,2},{5,4},{6,5},{7,6},{9,8},{10,9},{11,10},{13,12},{... | collective-permute-start | bytes 393224 | tf_op jit(solution)/shard_map/while/body/eval_jaxpr/ppermute | solution.py:18
  515.7 11.1 %collective-permute-start = (bf16[64,2,4,128]{3,0,2,1:T(8,128)(2,1)}, bf16[64,2,4,128]{3,0,2,1:T(8,128)(2,1)S(1)}, u32[]{:S(2)}, u32[]{:S(2)}) collective-permute-start(bf16[64,2,4,128]{3,0,2,1:T(8,128)(2,1)} %broadcast_select_fusion.4), channel_id=1, source_target_pairs={{0,32},{32,64},{64,96},{96,128},{128,160},{160,192},{192,224},{224... | collective-permute-start | bytes 393224 | tf_op jit(solution)/shard_map/while/body/eval_jaxpr/ppermute | solution.py:26
  517.7 10.5 %collective-permute-start.1 = (bf16[64,2,4,128]{3,0,2,1:T(8,128)(2,1)S(1)}, bf16[64,2,4,128]{3,0,2,1:T(8,128)(2,1)S(1)}, u32[]{:S(2)}, u32[]{:S(2)}) collective-permute-start(bf16[64,2,4,128]{3,0,2,1:T(8,128)(2,1)S(1)} %broadcast_select_fusion.5), channel_id=1, source_target_pairs={{32,0},{64,32},{96,64},{128,96},{160,128},{192,160},{224,192},{256... | collective-permute-start | bytes 393224 | tf_op jit(solution)/shard_map/while/body/eval_jaxpr/ppermute | solution.py:26
  530.8 8.1 %collective-permute-start.3 = (bf16[128,1,4,128]{3,0,2,1:T(8,128)(2,1)S(1)}, bf16[128,1,4,128]{3,0,2,1:T(8,128)(2,1)S(1)}, u32[]{:S(2)}, u32[]{:S(2)}) collective-permute-start(bf16[128,1,4,128]{3,0,2,1:T(8,128)(2,1)S(1)} %get-tuple-element.364), channel_id=1, source_target_pairs={{0,4},{4,8},{8,12},{12,16},{16,20},{20,24},{24,28},{1,5},{5,9},{9,... | collective-permute-start | bytes 393224 | tf_op jit(solution)/shard_map/while/body/eval_jaxpr/ppermute | solution.py:17
  538.9 8.8 %collective-permute-start.4 = (bf16[128,4,1,128]{3,0,2,1:T(8,128)(2,1)S(1)}, bf16[128,4,1,128]{3,0,2,1:T(8,128)(2,1)S(1)}, u32[]{:S(2)}, u32[]{:S(2)}) collective-permute-start(bf16[128,4,1,128]{3,0,2,1:T(8,128)(2,1)S(1)} %get-tuple-element.365), channel_id=1, source_target_pairs={{1,0},{2,1},{3,2},{5,4},{6,5},{7,6},{9,8},{10,9},{11,10},{13,12},{... | collective-permute-start | bytes 393224 | tf_op jit(solution)/shard_map/while/body/eval_jaxpr/ppermute | solution.py:18
  (34 other events, 213.0 us)
where the time goes:
time: 634 us; the launch traced here: 630 us
  starting transfers between devices  325 us (51%)
  waiting for transfers between devices  147 us (23%)
  blocking collectives  78.3 us (12%)
  other arithmetic  35.9 us (6%)
  matrix products  35.1 us (6%)
    ppermute x32, starting transfers between devices, shifted(): return lax.ppermute(block, axis, route)  162 us
    ppermute x32, waiting for transfers between devices, extended(): before = lax.ppermute(last, axis, up)  105 us
    ppermute x32, starting transfers between devices, extended(): before = lax.ppermute(last, axis, up)  101 us
    psum x1, blocking collectives, local(): gradient = lax.psum(contribution, 'layer')  78.3 us
    ppermute x32, starting transfers between devices, extended(): after = lax.ppermute(initial, axis, down)  61.9 us
    dot_general x144, matrix products, apply_front(): jnp.einsum('pijc,ijcd->pijd', beside, front_blocks[:, :, offset], preferr...  34.3 us
    ppermute x32, waiting for transfers between devices, shifted(): return lax.ppermute(block, axis, route)  29.2 us
  transfers between devices with their start and end apart: 96, of which 80 were waited for; matrix products, arithmetic and copies ran while one was open for 5% of the time, Pallas kernels for 0%

commit v1 on v0

v1 whole, which is shorter than its diff:
```python
import functools

import jax
import jax.numpy as jnp
from jax import lax
from jax.experimental import pallas as pl
from jax.experimental.pallas import tpu as pltpu
from jax.sharding import PartitionSpec as P

port_strength = 4.0
intersection_scale = 0.125

LAYERS, ROWS, COLS = 16, 8, 4
TX, TY = 2, 4
PORTS, TILE, GROUPS = 64, 128, 4
CHUNK = 16
CHUNKS = PORTS // CHUNK
MESH = pl.DeviceIdType.MESH

BESIDE = [(-1, -1), (-1, 1), (1, -1), (1, 1), (-1, 0), (1, 0), (0, -1), (0, 1), (0, 0)]
MINE_X = {-1: pl.ds(0, 1), 0: pl.ds(0, 2), 1: pl.ds(1, 1)}
MINE_Y = {-1: pl.ds(0, 1), 0: pl.ds(0, 4), 1: pl.ds(3, 1)}
THERE_X = {-1: pl.ds(3, 1), 0: pl.ds(1, 2), 1: pl.ds(0, 1)}
THERE_Y = {-1: pl.ds(5, 1), 0: pl.ds(1, 4), 1: pl.ds(0, 1)}


def kernel(
    forward_rhs,
    adjoint_rhs,
    blocks,
    pattern,
    coupling,
    layer_group,
    fields,
    gradient,
    weights,
    framed,
    waves,
    coming,
    partial,
    mine,
    theirs,
    load_sem,
    send_sem,
    recv_sem,
    start_send,
    ahead_send,
    ahead_recv,
    sum_send,
    sum_recv,
):
    layer, row, col = (lax.axis_index(a) for a in ("layer", "row", "col"))
    first_layer, last_layer = layer == 0, layer == LAYERS - 1

    loading = pltpu.make_async_copy(blocks, weights, load_sem)
    loading.start()

    def beside(a, b):
        ok = None
        for cond in (
            [row > 0] if a < 0 else [row < ROWS - 1] if a > 0 else []
        ) + ([col > 0] if b < 0 else [col < COLS - 1] if b > 0 else []):
            ok = cond if ok is None else jnp.logical_and(ok, cond)
        return ok

    def when(*conds):
        conds = [c for c in conds if c is not None]
        return pl.when(functools.reduce(jnp.logical_and, conds)) if conds else (lambda f: f())

    def device(to_layer, a=0, b=0):
        return {"layer": to_layer, "row": row + a, "col": col + b}

    for edge, where in (
        (row == 0, (0, slice(None))),
        (row == ROWS - 1, (3, slice(None))),
        (col == 0, (slice(None), 0)),
        (col == COLS - 1, (slice(None), 5)),
    ):

        @pl.when(edge)
        def _(where=where):
            for s in range(2):
                for c in range(CHUNKS):
                    view = framed.at[(s, c) + where]
                    view[...] = jnp.zeros(view.shape, jnp.bfloat16)

    barrier = pltpu.get_barrier_semaphore()

    def greet(to_layer, a, b):
        pl.semaphore_signal(barrier, 1, device_id=device(to_layer, a, b), device_id_type=MESH)

    rows_beside = 3 - jnp.where(row == 0, 1, 0) - jnp.where(row == ROWS - 1, 1, 0)
    cols_beside = 3 - jnp.where(col == 0, 1, 0) - jnp.where(col == COLS - 1, 1, 0)
    edge_layer = jnp.where(jnp.logical_or(first_layer, last_layer), 1, 0)
    for a, b in BESIDE[:-1]:

        @when(beside(a, b), layer > 0)
        def _(a=a, b=b):
            greet(layer - 1, a, b)

        @when(beside(a, b), layer < LAYERS - 1)
        def _(a=a, b=b):
            greet(layer + 1, a, b)

        @when(beside(a, b), edge_layer == 1)
        def _(a=a, b=b):
            greet(layer, a, b)

    def greet_layer(k, _):
        greet(lax.rem(layer + k, LAYERS), 0, 0)
        return 0

    lax.fori_loop(1, LAYERS, greet_layer, 0)
    around = rows_beside * cols_beside - 1
    pl.semaphore_wait(barrier, LAYERS - 1 + around * 2)

    def ahead(s, c):
        return pltpu.make_async_remote_copy(
            src_ref=own(s, c),
            dst_ref=coming.at[s, :, :, pl.ds(c * CHUNK, CHUNK)],
            send_sem=ahead_send.at[s, c],
            recv_sem=ahead_recv.at[s, c],
            device_id=device(layer - 1 + 2 * s),
            device_id_type=MESH,
        )

    def hop(s, c, a, b, to_layer, source, sem):
        at = 3 * (a + 1) + b + 1
        return pltpu.make_async_remote_copy(
            src_ref=source.at[MINE_X[a], MINE_Y[b]],
            dst_ref=framed.at[s, c, THERE_X[a], THERE_Y[b]],
            send_sem=sem.at[c, at],
            recv_sem=recv_sem.at[s, c, at],
            device_id=device(to_layer, a, b),
            device_id_type=MESH,
        )

    def own(s, c):
        ports = pl.ds(pl.multiple_of(c * CHUNK, CHUNK), CHUNK)
        return (forward_rhs, adjoint_rhs)[s].at[:, :, ports]

    for s, starts in ((0, first_layer), (1, last_layer)):

        @pl.when(starts)
        def _(s=s):
            for c in range(CHUNKS):
                source = own(s, c)
                for a, b in BESIDE[:-1]:

                    @when(beside(a, b))
                    def _(a=a, b=b):
                        hop(s, c, a, b, layer, source, start_send).start()

                pltpu.make_async_copy(
                    source, framed.at[s, c, pl.ds(1, TX), pl.ds(1, TY)], recv_sem.at[s, c, 4]
                ).start()

    for s, sends in ((0, layer > 0), (1, layer < LAYERS - 1)):

        @pl.when(sends)
        def _(s=s):
            for c in range(CHUNKS):
                ahead(s, c).start()

    loading.wait()
    for i in range(TX):
        for j in range(TY):

            def mask(k, _, i=i, j=j):
                present = pattern[i, j, k].astype(jnp.float32).astype(jnp.bfloat16)
                weights[i, j, k] = weights[i, j, k] * present
                return 0

            lax.fori_loop(0, 9, mask, 0)

    partial[...] = jnp.zeros(partial.shape, jnp.float32)
    kappa_next = coupling[layer_group[jnp.minimum(layer + 1, LAYERS - 1)]]
    kappa_own = coupling[layer_group[layer]]

    late = jnp.where(layer < LAYERS // 2, 0, 1)

    def step(n, _):
        phase, c = n // CHUNKS, lax.rem(n, CHUNKS)
        s = lax.rem(phase + late, 2)
        to_layer = layer + 1 - 2 * s
        goes_on = jnp.where(s == 0, layer < LAYERS - 1, layer > 0)
        kappa = jnp.where(s == 0, kappa_next, kappa_own)
        ports = pl.ds(pl.multiple_of(c * CHUNK, CHUNK), CHUNK)

        @pl.when(goes_on)
        def _():
            pltpu.make_async_copy(
                coming.at[s, :, :, ports], coming.at[s, :, :, ports], ahead_recv.at[s, c]
            ).wait()

        for a, b in reversed(BESIDE):
            @when(beside(-a, -b))
            def _(a=a, b=b):
                landed = framed.at[s, c, THERE_X[a], THERE_Y[b]]
                pltpu.make_async_copy(
                    landed, landed, recv_sem.at[s, c, 3 * (a + 1) + b + 1]
                ).wait()

        for i in range(TX):
            for j in range(TY):
                lhs = jnp.concatenate(
                    [framed[s, c, i + k // 3, j + k % 3] for k in range(9)], axis=-1
                )
                rhs = weights[i, j].reshape(9 * TILE, TILE)
                field = jnp.dot(lhs, rhs, preferred_element_type=jnp.float32).astype(jnp.bfloat16)
                fields[s, i, j, ports] = field
                waves[s, c, i, j] = (
                    coming[s, i, j, ports].astype(jnp.float32) + kappa * field.astype(jnp.float32)
                ).astype(jnp.bfloat16)

        @pl.when(goes_on)
        def _():
            for a, b in BESIDE:

                @when(beside(a, b))
                def _(a=a, b=b):
                    hop(s, c, a, b, to_layer, waves.at[s, c], send_sem.at[s]).start()

        @pl.when(phase == 1)
        def _():
            for i in range(TX):
                for j in range(TY):
                    both = fields[0, i, j, ports].astype(jnp.float32) * fields[
                        1, i, j, ports
                    ].astype(jnp.float32)
                    partial[TY * i + j] += both

        return 0

    lax.fori_loop(0, 2 * CHUNKS, step, 0)

    for t in range(TX * TY):
        mine[pl.ds(t, 1)] = jnp.sum(partial[t], axis=0, keepdims=True) * intersection_scale

    def share(k):
        return pltpu.make_async_remote_copy(
            src_ref=mine,
            dst_ref=theirs.at[k],
            send_sem=sum_send.at[k],
            recv_sem=sum_recv.at[k],
            device_id=device(lax.rem(layer + k, LAYERS)),
            device_id_type=MESH,
        )

    def start_share(k, _):
        share(k).start()
        return 0

    lax.fori_loop(1, LAYERS, start_share, 0)
    theirs[0] = mine[...]

    for s, sends in ((0, layer > 0), (1, layer < LAYERS - 1)):

        @pl.when(sends)
        def _(s=s):
            for c in range(CHUNKS):
                ahead(s, c).wait_send()

    for s, starts, sends in ((0, first_layer, layer < LAYERS - 1), (1, last_layer, layer > 0)):

        def drain(c, _, s=s, sem=None):
            for a, b in BESIDE if sem is None else BESIDE[:-1]:

                @when(beside(a, b))
                def _(a=a, b=b):
                    out = send_sem.at[s] if sem is None else sem
                    hop(s, c, a, b, layer, waves.at[s, c], out).wait_send()

            return 0

        @pl.when(sends)
        def _(drain=drain):
            lax.fori_loop(0, CHUNKS, drain, 0)

        @pl.when(starts)
        def _(drain=drain):
            lax.fori_loop(0, CHUNKS, functools.partial(drain, sem=start_send), 0)

    def end_share(k, _):
        share(k).wait()
        return 0

    lax.fori_loop(1, LAYERS, end_share, 0)
    for g in range(GROUPS):

        def add(k, total, g=g):
            other = lax.rem(layer - k + LAYERS, LAYERS)
            chosen = jnp.where(layer_group[other] == g, 1.0, 0.0).astype(jnp.float32)
            return total + chosen * theirs[k]

        gradient[g] = lax.fori_loop(
            0, LAYERS, add, jnp.zeros((TX * TY, TILE), jnp.float32)
        )


def sweeps(forward_rhs, adjoint_rhs, blocks, pattern, coupling, layer_group):
    vmem, smem = (pl.BlockSpec(memory_space=m) for m in (pltpu.VMEM, pltpu.SMEM))
    return pl.pallas_call(
        kernel,
        out_shape=(
            jax.ShapeDtypeStruct((2, TX, TY, PORTS, TILE), jnp.bfloat16),
            jax.ShapeDtypeStruct((GROUPS, TX * TY, TILE), jnp.float32),
        ),
        in_specs=[vmem, vmem, pl.BlockSpec(memory_space=pl.ANY), smem, smem, smem],
        out_specs=(vmem, vmem),
        scratch_shapes=[
            pltpu.VMEM((TX, TY, 9, TILE, TILE), jnp.bfloat16),
            pltpu.VMEM((2, CHUNKS, TX + 2, TY + 2, CHUNK, TILE), jnp.bfloat16),
            pltpu.VMEM((2, CHUNKS, TX, TY, CHUNK, TILE), jnp.bfloat16),
            pltpu.VMEM((2, TX, TY, PORTS, TILE), jnp.bfloat16),
            pltpu.VMEM((TX * TY, CHUNK, TILE), jnp.float32),
            pltpu.VMEM((TX * TY, TILE), jnp.float32),
            pltpu.VMEM((LAYERS, TX * TY, TILE), jnp.float32),
            pltpu.SemaphoreType.DMA,
            pltpu.SemaphoreType.DMA((2, CHUNKS, 9)),
            pltpu.SemaphoreType.DMA((2, CHUNKS, 9)),
            pltpu.SemaphoreType.DMA((CHUNKS, 9)),
            pltpu.SemaphoreType.DMA((2, CHUNKS)),
            pltpu.SemaphoreType.DMA((2, CHUNKS)),
            pltpu.SemaphoreType.DMA((LAYERS,)),
            pltpu.SemaphoreType.DMA((LAYERS,)),
        ],
        compiler_params=pltpu.CompilerParams(
            collective_id=0, has_side_effects=True, vmem_limit_bytes=32 << 20
        ),
        name="sweeps",
    )(forward_rhs, adjoint_rhs, blocks, pattern, coupling, layer_group)


def local(sources, adjoint_sources, blocks, pattern, coupling, layer_group, port_cells):
    layer, row, col = (lax.axis_index(a) for a in ("layer", "row", "col"))
    x = row * TX + lax.broadcasted_iota(jnp.int32, (1, TX, TY, TILE), 1)
    y = col * TY + lax.broadcasted_iota(jnp.int32, (1, TX, TY, TILE), 2)
    cell = (x * (COLS * TY) + y) * TILE + lax.broadcasted_iota(jnp.int32, (1, TX, TY, TILE), 3)
    port_map = jnp.where(cell == port_cells[:, None, None, None], port_strength, 0.0)

    def rhs(array, flag):
        whole = array[0].astype(jnp.float32) + jnp.where(flag, 1.0, 0.0) * port_map
        return jnp.transpose(whole.astype(jnp.bfloat16), (1, 2, 0, 3))

    fields, gradient = sweeps(
        rhs(sources, layer == 0),
        rhs(adjoint_sources, layer == LAYERS - 1),
        blocks[0],
        pattern[0],
        coupling,
        layer_group,
    )
    fields = jnp.transpose(fields, (0, 3, 1, 2, 4))
    return (fields[:1], fields[1:], gradient.reshape(GROUPS, TX, TY, TILE))


def solution(mesh):
    placed = (
        P("layer", None, "row", "col", None),
        P("layer", None, "row", "col", None),
        P("layer", "row", "col", None, None, None),
        P("layer", "row", "col", None),
        P(),
        P(),
        P(),
    )
    return jax.shard_map(
        local,
        mesh=mesh,
        in_specs=placed,
        out_specs=(
            P("layer", None, "row", "col", None),
            P("layer", None, "row", "col", None),
            P(None, "row", "col", None),
        ),
        check_vma=False,
    )
```

time: 634 us -> 137 us (0.22)
  the two profiles are of different devices: /device:TPU:38 before, /device:TPU:32 now
where the time goes in v1:
time: 137 us
  Pallas kernels  129 us (94%)
  local copies, waits for them, and re-layouts  5.8 us (4%)
    pallas_call x1, Pallas kernels, sweeps(): pl.pallas_call(kernel, out_shape=(jax.ShapeDtypeStruct((2, TX, TY, PORTS,...  129 us
    unnamed x11, local copies, waits for them, and re-layouts  5.78 us

profile of v1, /device:TPU:32, one launch (start us, length us, event | category | flops | bytes accessed | tf_op | source)
XLA Modules:
  0.0 136.9 jit_solution(5976825181430826326)
XLA Ops:
  0.7 0.1 iota_add_fusion
  0.7 1.1 fusion.4
  1.9 0.0 copy-start
  1.9 1.7 %copy-done = bf16[1,2,4,9,128,128]{5,4,3,2,1,0:T(8,128)(2,1)S(1)} copy-done((bf16[1,2,4,9,128,128]{5,4,3,2,1,0:T(8,128)(2,1)S(1)}, bf16[1,2,4,9,128,128]{5,4,3,2,1,0:T(8,128)(2,1)}, u32[]{:S(2)}) %copy-start) | copy-done | bytes 2359320
  3.6 0.0 copy-start.1
  3.6 0.7 copy-done.1
  4.2 0.0 copy-start.2
  4.2 0.7 copy-done.2
  4.9 0.0 copy-start.3
  4.9 0.7 copy-done.3
  5.6 129.2 %sweeps.1 = (bf16[2,2,4,64,128]{4,3,2,1,0:T(8,128)(2,1)S(1)}, f32[4,8,128]{2,1,0:T(8,128)S(1)}) custom-call(bf16[2,4,64,128]{3,2,1,0:T(8,128)(2,1)S(1)} %get-tuple-element.13.forward_rhs, bf16[2,4,64,128]{3,2,1,0:T(8,128)(2,1)S(1)} %get-tuple-element.12.adjoint_rhs, bf16[2,4,9,128,128]{4,3,2,1,0:T(8,128)(2,1)S(1)} %bitcast.14, s32[2,4,9]{2,1,0:T(4,128)S(1)} %bitcast.17, ...), custom_call_target="tpu_custom_call" | custom-call | tf_op jit(solution)/shard_map/sweeps/pallas_call | solution.py:303
  134.8 0.8 copy.13
  135.5 0.8 copy.12
  136.3 0.6 copy.17
  (3 shorter events, 0.0 us)
Async XLA Ops:
  1.9 1.7 %copy-start = (bf16[1,2,4,9,128,128]{5,4,3,2,1,0:T(8,128)(2,1)S(1)}, bf16[1,2,4,9,128,128]{5,4,3,2,1,0:T(8,128)(2,1)}, u32[]{:S(2)}) copy-start(bf16[1,2,4,9,128,128]{5,4,3,2,1,0:T(8,128)(2,1)} %param.9) | copy-start | bytes 7077892
  3.6 0.7 copy-start.1
  4.2 0.7 copy-start.2
  4.9 0.7 copy-start.3

commit v2 on v1

v2 whole, which is shorter than its diff:
```python
import functools

import jax
import jax.numpy as jnp
from jax import lax
from jax.experimental import pallas as pl
from jax.experimental.pallas import tpu as pltpu
from jax.sharding import PartitionSpec as P

port_strength = 4.0
intersection_scale = 0.125

LAYERS, ROWS, COLS = 16, 8, 4
TX, TY = 2, 4
PORTS, TILE, GROUPS = 64, 128, 4
CHUNK = 8
CHUNKS = PORTS // CHUNK
LAG = 4
MESH = pl.DeviceIdType.MESH

UP = [(-1, -1), (-1, 1), (-1, 0)]
DOWN = [(1, -1), (1, 1), (1, 0)]
LEVEL = [(0, -1), (0, 1)]
BESIDE = UP + DOWN + LEVEL
MINE_X = {-1: pl.ds(0, 1), 0: pl.ds(0, 2), 1: pl.ds(1, 1)}
MINE_Y = {-1: pl.ds(0, 1), 0: pl.ds(0, 4), 1: pl.ds(3, 1)}
THERE_X = {-1: pl.ds(3, 1), 0: pl.ds(1, 2), 1: pl.ds(0, 1)}
THERE_Y = {-1: pl.ds(5, 1), 0: pl.ds(1, 4), 1: pl.ds(0, 1)}
OWN, ABOVE, ASIDE = 0, 1, 2


def kernel(
    forward_rhs,
    adjoint_rhs,
    blocks,
    pattern,
    coupling,
    layer_group,
    forward_field,
    adjoint_field,
    gradient,
    weights,
    framed,
    waves,
    fields,
    coming,
    partial,
    mine,
    theirs,
    load_sem,
    send_sem,
    recv_sem,
    start_send,
    ahead_send,
    ahead_recv,
    sum_send,
    sum_recv,
):
    layer, row, col = (lax.axis_index(a) for a in ("layer", "row", "col"))
    first_layer, last_layer = layer == 0, layer == LAYERS - 1

    loading = pltpu.make_async_copy(blocks, weights, load_sem)
    loading.start()

    def beside(a, b):
        conds = [[row > 0], [], [row < ROWS - 1]][a + 1] + [[col > 0], [], [col < COLS - 1]][b + 1]
        return functools.reduce(jnp.logical_and, conds) if conds else None

    def when(*conds):
        conds = [c for c in conds if c is not None]
        return pl.when(functools.reduce(jnp.logical_and, conds)) if conds else (lambda f: f())

    def device(to_layer, a=0, b=0):
        return {"layer": to_layer, "row": row + a, "col": col + b}

    barrier = pltpu.get_barrier_semaphore()

    def greet(to_layer, a, b):
        pl.semaphore_signal(barrier, 1, device_id=device(to_layer, a, b), device_id_type=MESH)

    row_edge = jnp.logical_or(row == 0, row == ROWS - 1)
    col_edge = jnp.logical_or(col == 0, col == COLS - 1)
    rows_beside = jnp.where(row_edge, 1, 2)
    cols_beside = jnp.where(col_edge, 1, 2)
    for a, b in BESIDE:

        @when(beside(a, b))
        def _(a=a, b=b):
            greet(jnp.where(first_layer, 0, layer - 1), a, b)
            greet(jnp.where(last_layer, layer, layer + 1), a, b)

    def greet_layer(k, _):
        greet(lax.rem(layer + k, LAYERS), 0, 0)
        return 0

    lax.fori_loop(1, LAYERS, greet_layer, 0)

    for edge, where in (
        (row == 0, (0, slice(None))),
        (row == ROWS - 1, (TX + 1, slice(None))),
        (col == 0, (slice(None), 0)),
        (col == COLS - 1, (slice(None), TY + 1)),
    ):

        @pl.when(edge)
        def _(where=where):
            def clear(n, _):
                view = framed.at[(n // CHUNKS, lax.rem(n, CHUNKS)) + where]
                view[...] = jnp.zeros(view.shape, jnp.bfloat16)
                return 0

            lax.fori_loop(0, 2 * CHUNKS, clear, 0)

    loading.wait()
    for i in range(TX):
        for j in range(TY):

            def mask(k, _, i=i, j=j):
                present = pattern[i, j, k].astype(jnp.float32).astype(jnp.bfloat16)
                weights[i, j, k] = weights[i, j, k] * present
                return 0

            lax.fori_loop(0, 9, mask, 0)

    partial[...] = jnp.zeros(partial.shape, jnp.float32)
    pl.semaphore_wait(barrier, LAYERS - 1 + ((rows_beside + 1) * (cols_beside + 1) - 1) * 2)

    def own(s, c):
        return (forward_rhs, adjoint_rhs)[s].at[
            :, :, pl.ds(pl.multiple_of(c * CHUNK, CHUNK), CHUNK)
        ]

    def ahead(s, c):
        return pltpu.make_async_remote_copy(
            src_ref=own(s, c),
            dst_ref=coming.at[s, c],
            send_sem=ahead_send.at[s],
            recv_sem=ahead_recv.at[s, c],
            device_id=device(layer - 1 + 2 * s),
            device_id_type=MESH,
        )

    def hop(s, c, a, b, to_layer, source, sem):
        kind = ABOVE if a else ASIDE if b else OWN
        return pltpu.make_async_remote_copy(
            src_ref=source.at[MINE_X[a], MINE_Y[b]],
            dst_ref=framed.at[s, c, THERE_X[a], THERE_Y[b]],
            send_sem=sem,
            recv_sem=recv_sem.at[s, c, kind],
            device_id=device(to_layer, a, b),
            device_id_type=MESH,
        )

    def hops(offsets, s, c, to_layer, source, sem):
        for a, b in offsets:

            @when(beside(a, b))
            def _(a=a, b=b):
                hop(s, c, a, b, to_layer, source, sem).start()

    for s, starts in ((0, first_layer), (1, last_layer)):

        @pl.when(starts)
        def _(s=s):
            def begin(c, _):
                hops(UP + DOWN, s, c, layer, own(s, c), start_send.at[0])
                hops(LEVEL, s, c, layer, own(s, c), start_send.at[1])
                pltpu.make_async_copy(
                    own(s, c), framed.at[s, c, pl.ds(1, TX), pl.ds(1, TY)], recv_sem.at[s, c, OWN]
                ).start()
                return 0

            lax.fori_loop(0, CHUNKS, begin, 0)

    for s, sends in ((0, layer > 0), (1, layer < LAYERS - 1)):

        @pl.when(sends)
        def _(s=s):
            for c in range(CHUNKS):
                ahead(s, c).start()

    kappa_next = coupling[layer_group[jnp.minimum(layer + 1, LAYERS - 1)]]
    kappa_own = coupling[layer_group[layer]]
    late = jnp.where(layer < LAYERS // 2, 0, 1)
    middle = jnp.logical_or(layer == LAYERS // 2 - 1, layer == LAYERS // 2)
    lag = jnp.where(middle, min(LAG, CHUNKS), CHUNKS)

    def await_bytes(view, sem):
        pltpu.make_async_copy(view, view, sem).wait()

    def by_edges(f):
        for on_row_edge in (False, True):
            for on_col_edge in (False, True):

                @pl.when(jnp.logical_and(row_edge == on_row_edge, col_edge == on_col_edge))
                def _(r=1 if on_row_edge else 2, c=1 if on_col_edge else 2):
                    f(r, c)

    def products(s, c, i, j, ks):
        lhs = jnp.concatenate([framed[s, c, i + k // 3, j + k % 3] for k in ks], axis=-1)
        rhs = jnp.concatenate([weights[i, j, k] for k in ks], axis=0)
        return jnp.dot(lhs, rhs, preferred_element_type=jnp.float32)

    inside = {
        (i, j): [
            k for k in range(9) if 0 <= i + k // 3 - 1 < TX and 0 <= j + k % 3 - 1 < TY
        ]
        for i in range(TX)
        for j in range(TY)
    }

    def step(n, _):
        turn = n - lag
        mixed = jnp.logical_and(turn >= 0, n < 2 * CHUNKS - lag)
        phase = jnp.where(turn < 0, 0, jnp.where(mixed, lax.rem(turn, 2), 1))
        c = jnp.where(
            turn < 0, n, jnp.where(mixed, turn // 2 + jnp.where(phase == 0, lag, 0), n - CHUNKS)
        )
        s = lax.rem(phase + late, 2)
        to_layer = layer + 1 - 2 * s
        goes_on = jnp.where(s == 0, layer < LAYERS - 1, layer > 0)
        kappa = jnp.where(s == 0, kappa_next, kappa_own)

        @pl.when(goes_on)
        def _():
            await_bytes(coming.at[s, c], ahead_recv.at[s, c])

        await_bytes(framed.at[s, c, pl.ds(1, TX), pl.ds(1, TY)], recv_sem.at[s, c, OWN])
        sums = {ij: products(s, c, *ij, ks) for ij, ks in inside.items()}

        @by_edges
        def _(rows, cols):
            await_bytes(
                framed.at[s, c, pl.ds(0, rows), pl.ds(0, TY + cols)], recv_sem.at[s, c, ABOVE]
            )
            await_bytes(framed.at[s, c, pl.ds(0, TX), pl.ds(0, cols)], recv_sem.at[s, c, ASIDE])

        for i in range(TX):
            for j in range(TY):
                outside = [k for k in range(9) if k not in inside[i, j]]
                field = (sums[i, j] + products(s, c, i, j, outside)).astype(jnp.bfloat16)
                fields[s, c, i, j] = field
                waves[s, c, i, j] = (
                    coming[s, c, i, j].astype(jnp.float32) + kappa * field.astype(jnp.float32)
                ).astype(jnp.bfloat16)

            @pl.when(goes_on)
            def _(i=i):
                hops(
                    UP if i == 0 else DOWN + LEVEL + [(0, 0)],
                    s,
                    c,
                    to_layer,
                    waves.at[s, c],
                    send_sem.at[s],
                )

        @pl.when(phase == 1)
        def _():
            for i in range(TX):
                for j in range(TY):
                    both = fields[0, c, i, j].astype(jnp.float32) * fields[1, c, i, j].astype(
                        jnp.float32
                    )
                    partial[TY * i + j] += both

        return 0

    lax.fori_loop(0, 2 * CHUNKS, step, 0)

    for t in range(TX * TY):
        mine[pl.ds(t, 1)] = jnp.sum(partial[t], axis=0, keepdims=True) * intersection_scale

    def share(k):
        return pltpu.make_async_remote_copy(
            src_ref=mine,
            dst_ref=theirs.at[k],
            send_sem=sum_send,
            recv_sem=sum_recv,
            device_id=device(lax.rem(layer + k, LAYERS)),
            device_id_type=MESH,
        )

    def start_share(k, _):
        share(k).start()
        return 0

    lax.fori_loop(1, LAYERS, start_share, 0)
    theirs[0] = mine[...]

    for c in range(CHUNKS):
        forward_field[:, :, pl.ds(c * CHUNK, CHUNK)] = fields[0, c]
        adjoint_field[:, :, pl.ds(c * CHUNK, CHUNK)] = fields[1, c]

    for s, starts, stops in ((0, first_layer, last_layer), (1, last_layer, first_layer)):

        @pl.when(jnp.logical_not(starts))
        def _(s=s):
            await_bytes(coming.at[s], ahead_send.at[s])

        @by_edges
        def _(rows, cols, s=s, starts=starts, stops=stops):
            @pl.when(jnp.logical_not(stops))
            def _():
                await_bytes(
                    framed.at[s, :, pl.ds(0, TX + rows), pl.ds(0, TY + cols)], send_sem.at[s]
                )

            @pl.when(starts)
            def _():
                await_bytes(framed.at[s, :, pl.ds(0, rows), pl.ds(0, TY + cols)], start_send.at[0])
                await_bytes(framed.at[s, :, pl.ds(0, TX), pl.ds(0, cols)], start_send.at[1])

    others = theirs.at[pl.ds(1, LAYERS - 1)]
    await_bytes(others, sum_send)
    await_bytes(others, sum_recv)
    for g in range(GROUPS):

        def add(k, total, g=g):
            other = lax.rem(layer - k + LAYERS, LAYERS)
            chosen = jnp.where(layer_group[other] == g, 1.0, 0.0).astype(jnp.float32)
            return total + chosen * theirs[k]

        gradient[g] = lax.fori_loop(0, LAYERS, add, jnp.zeros((TX * TY, TILE), jnp.float32))


def sweeps(forward_rhs, adjoint_rhs, blocks, pattern, coupling, layer_group):
    vmem, smem = (pl.BlockSpec(memory_space=m) for m in (pltpu.VMEM, pltpu.SMEM))
    field = jax.ShapeDtypeStruct((TX, TY, PORTS, TILE), jnp.bfloat16)
    return pl.pallas_call(
        kernel,
        out_shape=(
            field,
            field,
            jax.ShapeDtypeStruct((GROUPS, TX * TY, TILE), jnp.float32),
        ),
        in_specs=[vmem, vmem, pl.BlockSpec(memory_space=pl.ANY), smem, smem, smem],
        out_specs=(vmem, vmem, vmem),
        scratch_shapes=[
            pltpu.VMEM((TX, TY, 9, TILE, TILE), jnp.bfloat16),
            pltpu.VMEM((2, CHUNKS, TX + 2, TY + 2, CHUNK, TILE), jnp.bfloat16),
            pltpu.VMEM((2, CHUNKS, TX, TY, CHUNK, TILE), jnp.bfloat16),
            pltpu.VMEM((2, CHUNKS, TX, TY, CHUNK, TILE), jnp.bfloat16),
            pltpu.VMEM((2, CHUNKS, TX, TY, CHUNK, TILE), jnp.bfloat16),
            pltpu.VMEM((TX * TY, CHUNK, TILE), jnp.float32),
            pltpu.VMEM((TX * TY, TILE), jnp.float32),
            pltpu.VMEM((LAYERS, TX * TY, TILE), jnp.float32),
            pltpu.SemaphoreType.DMA,
            pltpu.SemaphoreType.DMA((2,)),
            pltpu.SemaphoreType.DMA((2, CHUNKS, 3)),
            pltpu.SemaphoreType.DMA((2,)),
            pltpu.SemaphoreType.DMA((2,)),
            pltpu.SemaphoreType.DMA((2, CHUNKS)),
            pltpu.SemaphoreType.DMA,
            pltpu.SemaphoreType.DMA,
        ],
        compiler_params=pltpu.CompilerParams(
            collective_id=0, has_side_effects=True, vmem_limit_bytes=60 << 20
        ),
        name="sweeps",
    )(forward_rhs, adjoint_rhs, blocks, pattern, coupling, layer_group)


def local(sources, adjoint_sources, blocks, pattern, coupling, layer_group, port_cells):
    layer, row, col = (lax.axis_index(a) for a in ("layer", "row", "col"))
    x = row * TX + lax.broadcasted_iota(jnp.int32, (1, TX, TY, TILE), 1)
    y = col * TY + lax.broadcasted_iota(jnp.int32, (1, TX, TY, TILE), 2)
    cell = (x * (COLS * TY) + y) * TILE + lax.broadcasted_iota(jnp.int32, (1, TX, TY, TILE), 3)
    port_map = jnp.where(cell == port_cells[:, None, None, None], port_strength, 0.0)

    def rhs(array, flag):
        whole = array[0].astype(jnp.float32) + jnp.where(flag, 1.0, 0.0) * port_map
        return jnp.transpose(whole.astype(jnp.bfloat16), (1, 2, 0, 3))

    forward_field, adjoint_field, gradient = sweeps(
        rhs(sources, layer == 0),
        rhs(adjoint_sources, layer == LAYERS - 1),
        blocks[0],
        pattern[0],
        coupling,
        layer_group,
    )
    return (
        jnp.transpose(forward_field, (2, 0, 1, 3))[None],
        jnp.transpose(adjoint_field, (2, 0, 1, 3))[None],
        gradient.reshape(GROUPS, TX, TY, TILE),
    )


def solution(mesh):
    placed = (
        P("layer", None, "row", "col", None),
        P("layer", None, "row", "col", None),
        P("layer", "row", "col", None, None, None),
        P("layer", "row", "col", None),
        P(),
        P(),
        P(),
    )
    return jax.shard_map(
        local,
        mesh=mesh,
        in_specs=placed,
        out_specs=(
            P("layer", None, "row", "col", None),
            P("layer", None, "row", "col", None),
            P(None, "row", "col", None),
        ),
        check_vma=False,
    )
```

time: 137 us -> 110 us (0.80)
  the two profiles are of different devices: /device:TPU:32 before, /device:TPU:1 now
where the time goes in v2:
time: 110 us; the launch traced here: 109 us
  Pallas kernels  102 us (93%)
  local copies, waits for them, and re-layouts  4.65 us (4%)
  other arithmetic  1.92 us (2%)
    pallas_call x1, Pallas kernels, sweeps(): pl.pallas_call(kernel, out_shape=(field, field, jax.ShapeDtypeStruct((GRO...  102 us
    unnamed x3, local copies, waits for them, and re-layouts  4.65 us

profile of v2, /device:TPU:1, one launch (start us, length us, event | category | flops | bytes accessed | tf_op | source)
XLA Modules:
  0.0 109.5 jit_solution(3527715547042141657)
XLA Ops:
  0.7 0.1 iota_add_fusion
  0.7 1.8 %fusion.4 = (bf16[2,4,64,128]{3,2,1,0:T(8,128)(2,1)}, bf16[2,4,64,128]{3,2,1,0:T(8,128)(2,1)}) fusion(bf16[1,64,2,4,128]{4,3,2,1,0:T(4,128)(2,1)} %param.8, f32[]{:T(128)S(6)} %select_n.13, s32[2,4,128]{2,1,0:T(4,128)S(1)} %iota_add_fusion, s32[64]{0:T(128)} %param.13, f32[]{:T(128)S(6)} %select_n.11, bf16[1,64,2,4,128]{4,3,2,1,0:T(4,128)(2,1)} %param.7), kind=kLoop, calls=%fused_computation.6 | loop fusion | flops 655360 | bytes 528648 | tf_op jit(solution)/shard_map/transpose | solution.py:373
  2.6 102.2 %sweeps.1 = (bf16[2,4,64,128]{3,2,1,0:T(8,128)(2,1)}, bf16[2,4,64,128]{3,2,1,0:T(8,128)(2,1)}, f32[4,8,128]{2,1,0:T(8,128)}) custom-call(bf16[2,4,64,128]{3,2,1,0:T(8,128)(2,1)} %get-tuple-element.13.forward_rhs, bf16[2,4,64,128]{3,2,1,0:T(8,128)(2,1)} %get-tuple-element.12.adjoint_rhs, bf16[2,4,9,128,128]{4,3,2,1,0:T(8,128)(2,1)} %bitcast.19, ...), custom_call_target="tpu_custom_call" | custom-call | tf_op jit(solution)/shard_map/sweeps/pallas_call | solution.py:330
  104.8 1.7 %copy.12 = bf16[1,64,2,4,128]{4,3,2,1,0:T(4,128)(2,1)} copy(bf16[1,64,2,4,128]{4,1,3,2,0:T(8,128)(2,1)} %bitcast.21) | data formatting | bytes 262144
  106.5 1.7 %copy.13 = bf16[1,64,2,4,128]{4,3,2,1,0:T(4,128)(2,1)} copy(bf16[1,64,2,4,128]{4,1,3,2,0:T(8,128)(2,1)} %bitcast.20) | data formatting | bytes 262144
  108.2 1.3 %copy.17 = f32[4,2,4,128]{3,2,1,0:T(4,128)} copy(f32[4,2,4,128]{3,2,1,0:T(4,128)} %bitcast.22) | data formatting | bytes 32768
  (2 shorter events, 0.0 us)

commit v3 on v2

--- a/solution.py
+++ b/solution.py
@@ -30,15 +30,19 @@
 
 
 def kernel(
-    forward_rhs,
-    adjoint_rhs,
+    sources,
+    adjoint_sources,
     blocks,
     pattern,
     coupling,
     layer_group,
+    port_cells,
     forward_field,
     adjoint_field,
     gradient,
+    raw,
+    ready,
+    ported,
     weights,
     framed,
     waves,
@@ -48,6 +52,8 @@
     mine,
     theirs,
     load_sem,
+    raw_sem,
+    out_sem,
     send_sem,
     recv_sem,
     start_send,
@@ -61,6 +67,9 @@
 
     loading = pltpu.make_async_copy(blocks, weights, load_sem)
     loading.start()
+    late = jnp.where(layer < LAYERS // 2, 0, 1)
+    for s in range(2):
+        pltpu.make_async_copy((sources, adjoint_sources)[s], raw.at[s], raw_sem.at[s]).start()
 
     def beside(a, b):
         conds = [[row > 0], [], [row < ROWS - 1]][a + 1] + [[col > 0], [], [col < COLS - 1]][b + 1]
@@ -111,24 +120,34 @@
 
             lax.fori_loop(0, 2 * CHUNKS, clear, 0)
 
-    loading.wait()
-    for i in range(TX):
-        for j in range(TY):
-
-            def mask(k, _, i=i, j=j):
-                present = pattern[i, j, k].astype(jnp.float32).astype(jnp.bfloat16)
-                weights[i, j, k] = weights[i, j, k] * present
-                return 0
-
-            lax.fori_loop(0, 9, mask, 0)
-
+    tile = lax.broadcasted_iota(jnp.int32, (TX * TY, TILE), 0)
+    cell = (
+        (row * TX + tile // TY) * (COLS * TY) + col * TY + lax.rem(tile, TY)
+    ) * TILE + lax.broadcasted_iota(jnp.int32, (TX * TY, TILE), 1)
+
+    def prepare(s):
+        pltpu.make_async_copy(raw.at[s], raw.at[s], raw_sem.at[s]).wait()
+        starts = jnp.where(s == 0, first_layer, last_layer)
+        strength = jnp.where(starts, port_strength, 0.0).astype(jnp.float32)
+
+        def one(c, _):
+            at = pl.multiple_of(c * CHUNK, CHUNK)
+            whole = raw[s, pl.ds(at, CHUNK)].astype(jnp.float32)
+            ports = [jnp.where(cell == port_cells[at + p], strength, 0.0) for p in range(CHUNK)]
+            by_tile = jnp.swapaxes(whole + jnp.stack(ports), 0, 1).astype(jnp.bfloat16)
+            for i in range(TX):
+                for j in range(TY):
+                    ready[s, c, i, j] = by_tile[TY * i + j]
+            return 0
+
+        lax.fori_loop(0, CHUNKS, one, 0)
+
+    prepare(late)
     partial[...] = jnp.zeros(partial.shape, jnp.float32)
     pl.semaphore_wait(barrier, LAYERS - 1 + ((rows_beside + 1) * (cols_beside + 1) - 1) * 2)
 
     def own(s, c):
-        return (forward_rhs, adjoint_rhs)[s].at[
-            :, :, pl.ds(pl.multiple_of(c * CHUNK, CHUNK), CHUNK)
-        ]
+        return ready.at[s, c]
 
     def ahead(s, c):
         return pltpu.make_async_remote_copy(
@@ -172,16 +191,29 @@
 
             lax.fori_loop(0, CHUNKS, begin, 0)
 
-    for s, sends in ((0, layer > 0), (1, layer < LAYERS - 1)):
-
-        @pl.when(sends)
-        def _(s=s):
+    def send_ahead(s):
+        @pl.when(jnp.where(s == 0, layer > 0, layer < LAYERS - 1))
+        def _():
             for c in range(CHUNKS):
                 ahead(s, c).start()
 
+    send_ahead(late)
+    prepare(1 - late)
+    send_ahead(1 - late)
+
+    loading.wait()
+    for i in range(TX):
+        for j in range(TY):
+
+            def mask(k, _, i=i, j=j):
+                present = pattern[i, j, k].astype(jnp.float32).astype(jnp.bfloat16)
+                weights[i, j, k] = weights[i, j, k] * present
+                return 0
+
+            lax.fori_loop(0, 9, mask, 0)
+
     kappa_next = coupling[layer_group[jnp.minimum(layer + 1, LAYERS - 1)]]
     kappa_own = coupling[layer_group[layer]]
-    late = jnp.where(layer < LAYERS // 2, 0, 1)
     middle = jnp.logical_or(layer == LAYERS // 2 - 1, layer == LAYERS // 2)
     lag = jnp.where(middle, min(LAG, CHUNKS), CHUNKS)
 
@@ -235,11 +267,13 @@
             )
             await_bytes(framed.at[s, c, pl.ds(0, TX), pl.ds(0, cols)], recv_sem.at[s, c, ASIDE])
 
+        whole = []
         for i in range(TX):
             for j in range(TY):
                 outside = [k for k in range(9) if k not in inside[i, j]]
                 field = (sums[i, j] + products(s, c, i, j, outside)).astype(jnp.bfloat16)
                 fields[s, c, i, j] = field
+                whole.append(field.astype(jnp.float32))
                 waves[s, c, i, j] = (
                     coming[s, c, i, j].astype(jnp.float32) + kappa * field.astype(jnp.float32)
                 ).astype(jnp.bfloat16)
@@ -255,6 +289,16 @@
                     send_sem.at[s],
                 )
 
+        ports = pl.ds(pl.multiple_of(c * CHUNK, CHUNK), CHUNK)
+        ported[s, ports] = jnp.swapaxes(jnp.stack(whole), 0, 1).astype(jnp.bfloat16)
+        for sweep, out in ((0, forward_field), (1, adjoint_field)):
+
+            @pl.when(s == sweep)
+            def _(sweep=sweep, out=out):
+                pltpu.make_async_copy(
+                    ported.at[sweep, ports], out.at[ports], out_sem.at[sweep]
+                ).start()
+
         @pl.when(phase == 1)
         def _():
             for i in range(TX):
@@ -288,11 +332,9 @@
     lax.fori_loop(1, LAYERS, start_share, 0)
     theirs[0] = mine[...]
 
-    for c in range(CHUNKS):
-        forward_field[:, :, pl.ds(c * CHUNK, CHUNK)] = fields[0, c]
-        adjoint_field[:, :, pl.ds(c * CHUNK, CHUNK)] = fields[1, c]
-
     for s, starts, stops in ((0, first_layer, last_layer), (1, last_layer, first_layer)):
+
+        await_bytes(ported.at[s], out_sem.at[s])
 
         @pl.when(jnp.logical_not(starts))
         def _(s=s):
@@ -314,29 +356,33 @@
     others = theirs.at[pl.ds(1, LAYERS - 1)]
     await_bytes(others, sum_send)
     await_bytes(others, sum_recv)
+    totals = [jnp.zeros((TX * TY, TILE), jnp.float32)] * GROUPS
+    for k in range(LAYERS):
+        group = layer_group[lax.rem(layer - k + LAYERS, LAYERS)]
+        for g in range(GROUPS):
+            totals[g] += jnp.where(group == g, 1.0, 0.0).astype(jnp.float32) * theirs[k]
     for g in range(GROUPS):
-
-        def add(k, total, g=g):
-            other = lax.rem(layer - k + LAYERS, LAYERS)
-            chosen = jnp.where(layer_group[other] == g, 1.0, 0.0).astype(jnp.float32)
-            return total + chosen * theirs[k]
-
-        gradient[g] = lax.fori_loop(0, LAYERS, add, jnp.zeros((TX * TY, TILE), jnp.float32))
-
-
-def sweeps(forward_rhs, adjoint_rhs, blocks, pattern, coupling, layer_group):
-    vmem, smem = (pl.BlockSpec(memory_space=m) for m in (pltpu.VMEM, pltpu.SMEM))
-    field = jax.ShapeDtypeStruct((TX, TY, PORTS, TILE), jnp.bfloat16)
-    return pl.pallas_call(
+        gradient[g] = totals[g]
+
+
+def finish(*refs):
+    for a, b in zip(refs[:3], refs[3:]):
+        b[...] = a[...]
+
+
+def sweeps(*arguments):
+    vmem, smem, far = (pl.BlockSpec(memory_space=m) for m in (pltpu.VMEM, pltpu.SMEM, pl.ANY))
+    field = jax.ShapeDtypeStruct((PORTS, TX * TY, TILE), jnp.bfloat16)
+    outputs = (field, field, jax.ShapeDtypeStruct((GROUPS, TX * TY, TILE), jnp.float32))
+    results = pl.pallas_call(
         kernel,
-        out_shape=(
-            field,
-            field,
-            jax.ShapeDtypeStruct((GROUPS, TX * TY, TILE), jnp.float32),
-        ),
-        in_specs=[vmem, vmem, pl.BlockSpec(memory_space=pl.ANY), smem, smem, smem],
-        out_specs=(vmem, vmem, vmem),
+        out_shape=outputs,
+        in_specs=[far, far, far, smem, smem, smem, smem],
+        out_specs=(far, far, vmem),
         scratch_shapes=[
+            pltpu.VMEM((2, PORTS, TX * TY, TILE), jnp.bfloat16),
+            pltpu.VMEM((2, CHUNKS, TX, TY, CHUNK, TILE), jnp.bfloat16),
+            pltpu.VMEM((2, PORTS, TX * TY, TILE), jnp.bfloat16),
             pltpu.VMEM((TX, TY, 9, TILE, TILE), jnp.bfloat16),
             pltpu.VMEM((2, CHUNKS, TX + 2, TY + 2, CHUNK, TILE), jnp.bfloat16),
             pltpu.VMEM((2, CHUNKS, TX, TY, CHUNK, TILE), jnp.bfloat16),
@@ -346,6 +392,8 @@
             pltpu.VMEM((TX * TY, TILE), jnp.float32),
             pltpu.VMEM((LAYERS, TX * TY, TILE), jnp.float32),
             pltpu.SemaphoreType.DMA,
+            pltpu.SemaphoreType.DMA((2,)),
+            pltpu.SemaphoreType.DMA((2,)),
             pltpu.SemaphoreType.DMA((2,)),
             pltpu.SemaphoreType.DMA((2, CHUNKS, 3)),
             pltpu.SemaphoreType.DMA((2,)),
@@ -358,31 +406,29 @@
             collective_id=0, has_side_effects=True, vmem_limit_bytes=60 << 20
         ),
         name="sweeps",
-    )(forward_rhs, adjoint_rhs, blocks, pattern, coupling, layer_group)
+    )(*arguments)
+    return pl.pallas_call(
+        finish,
+        out_shape=outputs,
+        in_specs=[vmem] * 3,
+        out_specs=(vmem,) * 3,
+        name="finish",
+    )(*results)
 
 
 def local(sources, adjoint_sources, blocks, pattern, coupling, layer_group, port_cells):
-    layer, row, col = (lax.axis_index(a) for a in ("layer", "row", "col"))
-    x = row * TX + lax.broadcasted_iota(jnp.int32, (1, TX, TY, TILE), 1)
-    y = col * TY + lax.broadcasted_iota(jnp.int32, (1, TX, TY, TILE), 2)
-    cell = (x * (COLS * TY) + y) * TILE + lax.broadcasted_iota(jnp.int32, (1, TX, TY, TILE), 3)
-    port_map = jnp.where(cell == port_cells[:, None, None, None], port_strength, 0.0)
-
-    def rhs(array, flag):
-        whole = array[0].astype(jnp.float32) + jnp.where(flag, 1.0, 0.0) * port_map
-        return jnp.transpose(whole.astype(jnp.bfloat16), (1, 2, 0, 3))
-
     forward_field, adjoint_field, gradient = sweeps(
-        rhs(sources, layer == 0),
-        rhs(adjoint_sources, layer == LAYERS - 1),
+        sources.reshape(PORTS, TX * TY, TILE),
+        adjoint_sources.reshape(PORTS, TX * TY, TILE),
         blocks[0],
         pattern[0],
         coupling,
         layer_group,
+        port_cells,
     )
     return (
-        jnp.transpose(forward_field, (2, 0, 1, 3))[None],
-        jnp.transpose(adjoint_field, (2, 0, 1, 3))[None],
+        forward_field.reshape(1, PORTS, TX, TY, TILE),
+        adjoint_field.reshape(1, PORTS, TX, TY, TILE),
         gradient.reshape(GROUPS, TX, TY, TILE),
     )
 

time: 110 us -> 103 us (0.936)
  local copies, waits for them, and re-layouts: 4.65 us -> 0 us
  other arithmetic: 1.92 us -> 0 us
    unnamed x3 -> x0, local copies, waits for them, and re-layouts: 4.65 us -> none
    transpose x1 -> x0, other arithmetic: 1.84 us -> none  [rhs(): return jnp.transpose(whole.astype(jnp.bfloat16), (1, 2, 0, 3))]
    pallas_call x1 -> x2, Pallas kernels: 102 us -> 103 us  [the longest x1 101 us: sweeps(): pl.pallas_call(kernel, out_shape=outputs, in_specs=[far, far, far, smem,...]
where the time goes in v3:
time: 103 us
  Pallas kernels  103 us (100%)
    pallas_call x1, Pallas kernels, sweeps(): pl.pallas_call(kernel, out_shape=outputs, in_specs=[far, far, far, smem,...  101 us

profile of v3, /device:TPU:1, one launch (start us, length us, event | category | flops | bytes accessed | tf_op | source)
XLA Modules:
  0.0 103.2 jit_solution(13911548402174793741)
XLA Ops:
  0.6 100.9 %sweeps.1 = (bf16[64,8,128]{2,1,0:T(8,128)(2,1)}, bf16[64,8,128]{2,1,0:T(8,128)(2,1)}, f32[4,8,128]{2,1,0:T(8,128)}) custom-call(bf16[64,8,128]{2,1,0:T(8,128)(2,1)} %bitcast.8, bf16[64,8,128]{2,1,0:T(8,128)(2,1)} %bitcast.9, bf16[2,4,9,128,128]{4,3,2,1,0:T(8,128)(2,1)} %bitcast.7, s32[2,4,9]{2,1,0:T(4,128)} %bitcast.10, f32[4]{0:T(128)} %coupling.1, ...), custom_call_target="tpu_custom_call" | custom-call | tf_op jit(solution)/shard_map/sweeps/pallas_call | solution.py:377
  101.5 1.7 %finish.1 = (bf16[64,8,128]{2,1,0:T(8,128)(2,1)}, bf16[64,8,128]{2,1,0:T(8,128)(2,1)}, f32[4,8,128]{2,1,0:T(8,128)}) custom-call(bf16[64,8,128]{2,1,0:T(8,128)(2,1)} %get-tuple-element.9.refs_0_, bf16[64,8,128]{2,1,0:T(8,128)(2,1)} %get-tuple-element.10.refs_1_, f32[4,8,128]{2,1,0:T(8,128)} %get-tuple-element.11.refs_2_), custom_call_target="tpu_custom_call" | custom-call | tf_op jit(solution)/shard_map/finish/pallas_call | solution.py:410

commit v4 on v3

--- a/solution.py
+++ b/solution.py
@@ -26,7 +26,7 @@
 MINE_Y = {-1: pl.ds(0, 1), 0: pl.ds(0, 4), 1: pl.ds(3, 1)}
 THERE_X = {-1: pl.ds(3, 1), 0: pl.ds(1, 2), 1: pl.ds(0, 1)}
 THERE_Y = {-1: pl.ds(5, 1), 0: pl.ds(1, 4), 1: pl.ds(0, 1)}
-OWN, ABOVE, ASIDE = 0, 1, 2
+OWN, FRAME, ASIDE = 0, 1, 3
 
 
 def kernel(
@@ -160,7 +160,7 @@
         )
 
     def hop(s, c, a, b, to_layer, source, sem):
-        kind = ABOVE if a else ASIDE if b else OWN
+        kind = ASIDE if b else OWN
         return pltpu.make_async_remote_copy(
             src_ref=source.at[MINE_X[a], MINE_Y[b]],
             dst_ref=framed.at[s, c, THERE_X[a], THERE_Y[b]],
@@ -177,12 +177,29 @@
             def _(a=a, b=b):
                 hop(s, c, a, b, to_layer, source, sem).start()
 
+    def row_hops(i, s, c, to_layer, source, sem):
+        a = 2 * i - 1
+        there = jnp.logical_and(row + a >= 0, row + a < ROWS)
+        for b in (-1, 1, 0):
+
+            @when(there, beside(0, b))
+            def _(b=b):
+                pltpu.make_async_remote_copy(
+                    src_ref=source.at[pl.ds(i, 1), MINE_Y[b]],
+                    dst_ref=framed.at[s, c, pl.ds((TX + 1) * (1 - i), 1), THERE_Y[b]],
+                    send_sem=sem,
+                    recv_sem=recv_sem.at[s, c, FRAME + i],
+                    device_id=device(to_layer, a, b),
+                    device_id_type=MESH,
+                ).start()
+
     for s, starts in ((0, first_layer), (1, last_layer)):
 
         @pl.when(starts)
         def _(s=s):
             def begin(c, _):
-                hops(UP + DOWN, s, c, layer, own(s, c), start_send.at[0])
+                for i in range(TX):
+                    row_hops(i, s, c, layer, own(s, c), start_send.at[0])
                 hops(LEVEL, s, c, layer, own(s, c), start_send.at[1])
                 pltpu.make_async_copy(
                     own(s, c), framed.at[s, c, pl.ds(1, TX), pl.ds(1, TY)], recv_sem.at[s, c, OWN]
@@ -228,18 +245,25 @@
                 def _(r=1 if on_row_edge else 2, c=1 if on_col_edge else 2):
                     f(r, c)
 
-    def products(s, c, i, j, ks):
-        lhs = jnp.concatenate([framed[s, c, i + k // 3, j + k % 3] for k in ks], axis=-1)
-        rhs = jnp.concatenate([weights[i, j, k] for k in ks], axis=0)
-        return jnp.dot(lhs, rhs, preferred_element_type=jnp.float32)
-
-    inside = {
-        (i, j): [
-            k for k in range(9) if 0 <= i + k // 3 - 1 < TX and 0 <= j + k % 3 - 1 < TY
-        ]
-        for i in range(TX)
+    def products(s, c, i, j, terms):
+        lhs, rhs = [], []
+        for t, b in terms:
+            a = (2 * i - 1) * (1 - t)
+            lhs.append(framed[s, c, 1 + i + a, 1 + j + b])
+            rhs.append(weights[i, j, 3 * (a + 1) + b + 1])
+        return jnp.dot(
+            jnp.concatenate(lhs, axis=-1),
+            jnp.concatenate(rhs, axis=0),
+            preferred_element_type=jnp.float32,
+        )
+
+    inside = [
+        [(t, b) for t in (1, 2) for b in (-1, 0, 1) if 0 <= j + b < TY] for j in range(TY)
+    ]
+    outside = [
+        [(t, b) for t in range(3) for b in (-1, 0, 1) if (t, b) not in inside[j]]
         for j in range(TY)
-    }
+    ]
 
     def step(n, _):
         turn = n - lag
@@ -258,37 +282,42 @@
             await_bytes(coming.at[s, c], ahead_recv.at[s, c])
 
         await_bytes(framed.at[s, c, pl.ds(1, TX), pl.ds(1, TY)], recv_sem.at[s, c, OWN])
-        sums = {ij: products(s, c, *ij, ks) for ij, ks in inside.items()}
-
-        @by_edges
-        def _(rows, cols):
-            await_bytes(
-                framed.at[s, c, pl.ds(0, rows), pl.ds(0, TY + cols)], recv_sem.at[s, c, ABOVE]
-            )
-            await_bytes(framed.at[s, c, pl.ds(0, TX), pl.ds(0, cols)], recv_sem.at[s, c, ASIDE])
-
-        whole = []
-        for i in range(TX):
+        first = lax.rem(jnp.where(s == 0, layer, LAYERS - 1 - layer), 2)
+        order = (first, 1 - first)
+        sums = [[products(s, c, i, j, inside[j]) for j in range(TY)] for i in order]
+        for on_edge, cols in ((True, 1), (False, 2)):
+
+            @pl.when(col_edge == on_edge)
+            def _(cols=cols):
+                await_bytes(
+                    framed.at[s, c, pl.ds(0, TX), pl.ds(0, cols)], recv_sem.at[s, c, ASIDE]
+                )
+
+        for q, i in enumerate(order):
+            framing = jnp.where(i == 0, row > 0, row < ROWS - 1)
+            for on_edge, cols in ((True, 1), (False, 2)):
+
+                @pl.when(jnp.logical_and(framing, col_edge == on_edge))
+                def _(cols=cols, i=i):
+                    await_bytes(
+                        framed.at[s, c, pl.ds(0, 1), pl.ds(0, TY + cols)],
+                        recv_sem.at[s, c, FRAME + 1 - i],
+                    )
+
             for j in range(TY):
-                outside = [k for k in range(9) if k not in inside[i, j]]
-                field = (sums[i, j] + products(s, c, i, j, outside)).astype(jnp.bfloat16)
+                field = (sums[q][j] + products(s, c, i, j, outside[j])).astype(jnp.bfloat16)
                 fields[s, c, i, j] = field
-                whole.append(field.astype(jnp.float32))
                 waves[s, c, i, j] = (
                     coming[s, c, i, j].astype(jnp.float32) + kappa * field.astype(jnp.float32)
                 ).astype(jnp.bfloat16)
 
             @pl.when(goes_on)
-            def _(i=i):
-                hops(
-                    UP if i == 0 else DOWN + LEVEL + [(0, 0)],
-                    s,
-                    c,
-                    to_layer,
-                    waves.at[s, c],
-                    send_sem.at[s],
-                )
-
+            def _(q=q, i=i):
+                row_hops(i, s, c, to_layer, waves.at[s, c], send_sem.at[s])
+                if q == TX - 1:
+                    hops(LEVEL + [(0, 0)], s, c, to_layer, waves.at[s, c], send_sem.at[s])
+
+        whole = [fields[s, c, i, j].astype(jnp.float32) for i in range(TX) for j in range(TY)]
         ports = pl.ds(pl.multiple_of(c * CHUNK, CHUNK), CHUNK)
         ported[s, ports] = jnp.swapaxes(jnp.stack(whole), 0, 1).astype(jnp.bfloat16)
         for sweep, out in ((0, forward_field), (1, adjoint_field)):
@@ -395,7 +424,7 @@
             pltpu.SemaphoreType.DMA((2,)),
             pltpu.SemaphoreType.DMA((2,)),
             pltpu.SemaphoreType.DMA((2,)),
-            pltpu.SemaphoreType.DMA((2, CHUNKS, 3)),
+            pltpu.SemaphoreType.DMA((2, CHUNKS, 4)),
             pltpu.SemaphoreType.DMA((2,)),
             pltpu.SemaphoreType.DMA((2,)),
             pltpu.SemaphoreType.DMA((2, CHUNKS)),

time: 103 us -> 102 us (level); the launches traced: 103 us -> 101 us
  Pallas kernels: 103 us -> 100 us
    pallas_call x1, Pallas kernels: 101 us -> 98.6 us  [sweeps(): pl.pallas_call(kernel, out_shape=outputs, in_specs=[far, far, far, smem,...]
where the time goes in v4:
time: 102 us; the launch traced here: 101 us
  Pallas kernels  100 us (98%)
    pallas_call x1, Pallas kernels, sweeps(): pl.pallas_call(kernel, out_shape=outputs, in_specs=[far, far, far, smem,...  98.6 us

profile of v4, /device:TPU:1, one launch (start us, length us, event | category | flops | bytes accessed | tf_op | source)
XLA Modules:
  0.0 100.9 jit_solution(1078841914357629827)
XLA Ops:
  0.6 98.6 %sweeps.1 = (bf16[64,8,128]{2,1,0:T(8,128)(2,1)}, bf16[64,8,128]{2,1,0:T(8,128)(2,1)}, f32[4,8,128]{2,1,0:T(8,128)}) custom-call(bf16[64,8,128]{2,1,0:T(8,128)(2,1)} %bitcast.8, bf16[64,8,128]{2,1,0:T(8,128)(2,1)} %bitcast.9, bf16[2,4,9,128,128]{4,3,2,1,0:T(8,128)(2,1)} %bitcast.7, s32[2,4,9]{2,1,0:T(4,128)} %bitcast.10, f32[4]{0:T(128)} %coupling.1, ...), custom_call_target="tpu_custom_call" | custom-call | tf_op jit(solution)/shard_map/sweeps/pallas_call | solution.py:406
  99.3 1.7 %finish.1 = (bf16[64,8,128]{2,1,0:T(8,128)(2,1)}, bf16[64,8,128]{2,1,0:T(8,128)(2,1)}, f32[4,8,128]{2,1,0:T(8,128)}) custom-call(bf16[64,8,128]{2,1,0:T(8,128)(2,1)} %get-tuple-element.9.refs_0_, bf16[64,8,128]{2,1,0:T(8,128)(2,1)} %get-tuple-element.10.refs_1_, f32[4,8,128]{2,1,0:T(8,128)} %get-tuple-element.11.refs_2_), custom_call_target="tpu_custom_call" | custom-call | tf_op jit(solution)/shard_map/finish/pallas_call | solution.py:439

commit v5 on v4

--- a/solution.py
+++ b/solution.py
@@ -315,7 +315,15 @@
             def _(q=q, i=i):
                 row_hops(i, s, c, to_layer, waves.at[s, c], send_sem.at[s])
                 if q == TX - 1:
-                    hops(LEVEL + [(0, 0)], s, c, to_layer, waves.at[s, c], send_sem.at[s])
+                    hops(LEVEL, s, c, to_layer, waves.at[s, c], send_sem.at[s])
+                pltpu.make_async_remote_copy(
+                    src_ref=waves.at[s, c, pl.ds(i, 1)],
+                    dst_ref=framed.at[s, c, pl.ds(1 + i, 1), pl.ds(1, TY)],
+                    send_sem=send_sem.at[s],
+                    recv_sem=recv_sem.at[s, c, OWN],
+                    device_id=device(to_layer),
+                    device_id_type=MESH,
+                ).start()
 
         whole = [fields[s, c, i, j].astype(jnp.float32) for i in range(TX) for j in range(TY)]
         ports = pl.ds(pl.multiple_of(c * CHUNK, CHUNK), CHUNK)

time: 102 us -> 102 us (level)
  no operation moved by 1% of the time
where the time goes in v5:
time: 102 us
  Pallas kernels  101 us (99%)
    pallas_call x1, Pallas kernels, sweeps(): pl.pallas_call(kernel, out_shape=outputs, in_specs=[far, far, far, smem,...  99.6 us

profile of v5, /device:TPU:1, one launch (start us, length us, event | category | flops | bytes accessed | tf_op | source)
XLA Modules:
  0.0 101.9 jit_solution(15287603126258415846)
XLA Ops:
  0.6 99.6 %sweeps.1 = (bf16[64,8,128]{2,1,0:T(8,128)(2,1)}, bf16[64,8,128]{2,1,0:T(8,128)(2,1)}, f32[4,8,128]{2,1,0:T(8,128)}) custom-call(bf16[64,8,128]{2,1,0:T(8,128)(2,1)} %bitcast.8, bf16[64,8,128]{2,1,0:T(8,128)(2,1)} %bitcast.9, bf16[2,4,9,128,128]{4,3,2,1,0:T(8,128)(2,1)} %bitcast.7, s32[2,4,9]{2,1,0:T(4,128)} %bitcast.10, f32[4]{0:T(128)} %coupling.1, ...), custom_call_target="tpu_custom_call" | custom-call | tf_op jit(solution)/shard_map/sweeps/pallas_call | solution.py:414
  100.2 1.7 %finish.1 = (bf16[64,8,128]{2,1,0:T(8,128)(2,1)}, bf16[64,8,128]{2,1,0:T(8,128)(2,1)}, f32[4,8,128]{2,1,0:T(8,128)}) custom-call(bf16[64,8,128]{2,1,0:T(8,128)(2,1)} %get-tuple-element.9.refs_0_, bf16[64,8,128]{2,1,0:T(8,128)(2,1)} %get-tuple-element.10.refs_1_, f32[4,8,128]{2,1,0:T(8,128)} %get-tuple-element.11.refs_2_), custom_call_target="tpu_custom_call" | custom-call | tf_op jit(solution)/shard_map/finish/pallas_call | solution.py:447
